TPU v7x, 32 devices: a whole 2x2x4 slice. The times are simulated.
32 devices in a mesh: lat: 4 (over y, x), lon: 8 (over z, core).
Axes of the slice: x: 2, y: 2, z: 4, core: 2. Of those that a mesh axis runs over, the one named last changes fastest.
Arguments:
- control: float32 [548, 32, 1024], P(None, 'lat', 'lon'), may hold values from -6 to 6
- std_dev: float32 [548], replicated, may hold values from 0.3 to 3
- col_dev: int32 [3072, 1], P(('lat', 'lon')), may hold values from 0 to 31; in each aligned block of 96 rows (0 to 95, 96 to 191, ...) at most 6 rows name the same one
- col_cell: int32 [3072], P(('lat', 'lon')), may hold values from 0 to 1023
- jacobian: bfloat16 [3072, 150, 548], P(('lat', 'lon')), may hold values from -0.25 to 0.25
- innovation: float32 [3072, 150], P(('lat', 'lon')), may hold values from -6 to 6
- inv_error: float32 [150], replicated, may hold values from 0.3 to 3
Outputs:
- departures: float32 [3072, 150], P(('lat', 'lon'))
- increment: float32 [548, 32, 1024], P(None, 'lat', 'lon')
- adjoint: float32 [548, 32, 1024], P(None, 'lat', 'lon')
Inputs may be any that keep to these rules, and one draw needn't show every extreme that they name: `col_dev`: among the soundings of one device (aligned blocks of 96 rows) at most 6 name the same device, and in every draw some device is named exactly 6 times by one block.
All inputs are finite; a program needn't handle non-finite values.
Results may differ from a plain program's by a relative error of at most 0.0025.
Values may be sent and summed in bfloat16 or wider, within the bound.
A program may use at most 128 MiB of HBM per device.

v0:
```python
import functools

import jax
import jax.numpy as jnp
from jax import lax
from jax.experimental import pallas as pl
from jax.experimental.pallas import tpu as pltpu
from jax.sharding import PartitionSpec as P

LHALF = 8
HIGHEST = lax.Precision.HIGHEST


def tap_weights(offset, half_width):
    spread = 2.0 * half_width / 3.0
    taps = jnp.arange(-half_width, half_width + 1, dtype=jnp.int32).astype(jnp.float32)
    norm_total = jnp.sqrt(jnp.sum(jnp.exp(-taps * taps / (spread * spread))))
    weights = jnp.exp(-offset * offset / (2.0 * spread * spread)) / norm_total
    return jnp.where(jnp.abs(offset) <= half_width, weights, jnp.zeros_like(weights))


def band(out_count, in_count, half_width):
    row_index = jnp.arange(out_count, dtype=jnp.int32)[:, None]
    col_index = jnp.arange(in_count, dtype=jnp.int32)[None, :]
    return tap_weights((col_index - row_index - half_width).astype(jnp.float32), half_width)


def shifts(axis, wrap):
    peers = lax.axis_size(axis)
    up = [(i, (i + 1) % peers) for i in range(peers if wrap else peers - 1)]
    return up, [(j, i) for i, j in up]


def around(array, axis, wrap):
    up, down = shifts(axis, wrap)
    return lax.ppermute(array, axis, up), lax.ppermute(array, axis, down)


def halves(weights):
    high = weights.astype(jnp.bfloat16)
    return high, (weights - high.astype(jnp.float32)).astype(jnp.bfloat16)


def dot_split(data, weights):
    high, low = halves(weights)
    dot = lambda w: jnp.dot(data, w, preferred_element_type=jnp.float32)
    return dot(high) + dot(low)


def smooth(field, before, after):
    width, lat_rows, lon_cols = field.shape
    extended = jnp.concatenate([before.astype(jnp.float32), field, after.astype(jnp.float32)], axis=1)
    lat_band = band(lat_rows, lat_rows + 2 * LHALF, LHALF)
    field = jnp.einsum("ij,cjk->cik", lat_band, extended, precision=HIGHEST)
    lon_half, part = lon_cols // 2, width // 2
    rounded = field.astype(jnp.bfloat16)
    paired = lambda piece: jnp.concatenate([piece[:part], piece[part:]], axis=2)
    up, down = shifts("lon", True)
    left = lax.ppermute(paired(rounded[:, :, lon_half:]), "lon", up)
    right = lax.ppermute(paired(rounded[:, :, :lon_half]), "lon", down)
    lon_band = band(lon_cols, lon_cols + 2 * lon_half, lon_half).T
    edge = lambda w: jnp.concatenate(
        [jnp.concatenate([w, jnp.zeros_like(w)], 1), jnp.concatenate([jnp.zeros_like(w), w], 1)], 0
    )
    both = jnp.concatenate([left, right], axis=2).reshape(part * lat_rows, 2 * lon_cols)
    weights = jnp.concatenate([edge(lon_band[:lon_half]), edge(lon_band[-lon_half:])], 0)
    sides = dot_split(both, weights)
    sides = jnp.concatenate([sides[:, :lon_cols], sides[:, lon_cols:]], axis=0)
    own = jnp.dot(
        field.reshape(width * lat_rows, lon_cols), lon_band[lon_half:-lon_half], precision=HIGHEST
    )
    return (own + sides).reshape(width, lat_rows, lon_cols)


def lane_tiles(count):
    return -(-count // 128)


def fold_lanes(tile):
    rows, count = tile.shape
    total = tile[:, :128]
    for start in range(128, count, 128):
        total = total + tile[:, start : start + 128]
    return total


def sounding_kernel(channels, step, jac_ref, col_ref, innov_ref, inv_ref, dep_ref, grad_ref):
    rows, width = col_ref.shape
    lanes = lax.broadcasted_iota(jnp.int32, (rows, dep_ref.shape[1]), 1)
    columns = col_ref[...].astype(jnp.float32)
    dep_ref[...] = jnp.zeros_like(dep_ref)
    grad_ref[...] = jnp.zeros_like(grad_ref)

    def some(index, carry):
        weighted = []
        found = jnp.zeros(dep_ref.shape, jnp.float32)
        for k in range(step):
            channel = index * step + k
            product = jac_ref[channel].astype(jnp.float32) * columns
            departure = jnp.sum(product, axis=1, keepdims=True)
            departure = departure - jnp.sum(
                jnp.where(lanes == channel, innov_ref[...], 0.0), axis=1, keepdims=True
            )
            found = found + jnp.where(lanes == channel, departure, 0.0)
            weight = (departure * inv_ref[0, channel]).astype(jnp.bfloat16)
            weighted.append(weight.astype(jnp.float32))
        dep_ref[...] += found
        total = grad_ref[...]
        for k in range(step):
            total = total + jac_ref[index * step + k].astype(jnp.float32) * weighted[k]
        grad_ref[...] = total
        return carry

    lax.fori_loop(0, channels // step, some, 0)


def sounding_step(jacobian, columns, innovation, inv_error):
    count, channels, width = jacobian.shape
    rows = 16
    step = next(n for n in (10, 8, 6, 5, 4, 3, 2, 1) if channels % n == 0)
    padded = lane_tiles(channels) * 128
    innovation = jnp.pad(innovation, ((0, 0), (0, padded - channels)))
    departures, grad = pl.pallas_call(
        functools.partial(sounding_kernel, channels, step),
        grid=(count // rows,),
        in_specs=[
            pl.BlockSpec((channels, rows, width), lambda i: (0, i, 0)),
            pl.BlockSpec((rows, width), lambda i: (i, 0)),
            pl.BlockSpec((rows, padded), lambda i: (i, 0)),
            pl.BlockSpec(memory_space=pltpu.SMEM),
        ],
        out_specs=[
            pl.BlockSpec((rows, padded), lambda i: (i, 0)),
            pl.BlockSpec((rows, width), lambda i: (i, 0)),
        ],
        out_shape=[
            jax.ShapeDtypeStruct((count, padded), jnp.float32),
            jax.ShapeDtypeStruct((count, width), jnp.float32),
        ],
        name="soundings",
    )(jnp.transpose(jacobian, (1, 0, 2)), columns, innovation, inv_error[None, :])
    return departures[:, :channels], grad


def local(control, std_dev, col_dev, col_cell, jacobian, innovation, inv_error):
    width, lat_rows, lon_cols = control.shape
    devices = lax.axis_size("lat") * lax.axis_size("lon")
    sound_count = col_cell.shape[0]
    slots_each = max(2, 2 * sound_count // devices)
    slots = devices * slots_each

    before, after = around(control.astype(jnp.bfloat16), "lat", False)

    target = col_dev[:, 0]
    onehot = (target[:, None] == jnp.arange(devices, dtype=jnp.int32)[None, :]).astype(jnp.int32)
    below = jnp.arange(sound_count)[:, None] > jnp.arange(sound_count)[None, :]
    earlier = jnp.dot(
        below.astype(jnp.bfloat16), onehot.astype(jnp.bfloat16), preferred_element_type=jnp.float32
    ).astype(jnp.int32)
    order_in = jnp.sum(earlier * onehot, axis=1)
    slot = target * slots_each + order_in
    wanted = jnp.zeros((slots,), jnp.int32).at[slot].set(col_cell)
    requested = lax.all_to_all(
        wanted.reshape(devices, slots_each), ("lat", "lon"), split_axis=0, concat_axis=0, tiled=True
    ).reshape(-1)

    cells = jnp.stack([requested, *around(requested, "lat", False)])
    cells = jnp.stack([cells, *around(cells, "lon", True)]).reshape(3, 3, slots)
    shift = jnp.array([0, -1, 1], jnp.int32)
    rows = (cells // lon_cols + lat_rows * shift[None, :, None]).reshape(-1, 1)
    columns_at = (cells % lon_cols + lon_cols * shift[:, None, None]).reshape(-1, 1)
    row_weight = tap_weights((rows - jnp.arange(lat_rows)[None, :]).astype(jnp.float32), LHALF)
    col_weight = tap_weights((columns_at - jnp.arange(lon_cols)[None, :]).astype(jnp.float32), lon_cols // 2)
    spread = (row_weight[:, :, None] * col_weight[:, None, :]).reshape(-1, lat_rows * lon_cols)
    spread_high, spread_low = halves(spread)

    increment = smooth(control, before, after) * std_dev[:, None, None]
    flat_field = increment.reshape(width, lat_rows * lon_cols)
    picked = jnp.take(flat_field, requested, axis=1).T.astype(jnp.bfloat16)
    returned = lax.all_to_all(
        picked.reshape(devices, slots_each, width), ("lat", "lon"), split_axis=0, concat_axis=0, tiled=True
    )
    columns = returned.reshape(slots, width)[slot]
    departures, column_grad = sounding_step(jacobian, columns, innovation, inv_error)
    outgoing = jnp.zeros((slots, width), jnp.bfloat16).at[slot].set(column_grad.astype(jnp.bfloat16))
    arrived = lax.all_to_all(
        outgoing.reshape(devices, slots_each, width), ("lat", "lon"), split_axis=0, concat_axis=0, tiled=True
    ).reshape(slots, width)
    near = jnp.concatenate([arrived, *around(arrived, "lat", False)], axis=0)
    near = jnp.concatenate([near, *around(near, "lon", True)], axis=0)
    add_up = lambda w: lax.dot_general(
        near, w, (((0,), (0,)), ((), ())), preferred_element_type=jnp.float32
    )
    adjoint = (add_up(spread_high) + add_up(spread_low)) * std_dev[:, None]
    return (departures, increment, adjoint.reshape(width, lat_rows, lon_cols))


def solution(mesh):
    placed = (
        P(None, "lat", "lon"),
        P(),
        P(("lat", "lon"), None),
        P(("lat", "lon")),
        P(("lat", "lon"), None, None),
        P(("lat", "lon"), None),
        P(),
    )
    return jax.shard_map(
        local,
        mesh=mesh,
        in_specs=placed,
        out_specs=(P(("lat", "lon"), None), P(None, "lat", "lon"), P(None, "lat", "lon")),
        check_vma=False,
    )
```

profile of v0, /device:TPU:7, one launch (start us, length us, event | category | flops | bytes accessed | tf_op | source)
XLA Modules:
  0.0 193.9 jit_solution(6417914430116891986)
XLA Ops:
  0.6 1.7 convert_element_type.87
  2.4 2.2 %collective-permute-start.1 = (bf16[548,8,128]{2,1,0:T(8,128)(2,1)S(1)}, bf16[548,8,128]{2,1,0:T(8,128)(2,1)S(1)}, u32[]{:S(2)}, u32[]{:S(2)}) collective-permute-start(bf16[548,8,128]{2,1,0:T(8,128)(2,1)S(1)} %convert_element_type.87), channel_id=1, source_target_pairs={{8,0},{16,8},{24,16},{9,1},{17,9},{25,17},{10,2},{18,10},{26,18},{... | collective-permute-start | bytes 3366920 | tf_op jit(solution)/shard_map/ppermute | solution.py:36
  7.8 8.6 %all-to-all-start = ((s32[32,1,6]{2,1,0:T(1,128)}), s32[32,1,6]{2,1,0:T(1,128)S(1)}, u32[]{:S(2)}, u32[]{:S(2)}) async-start(s32[32,1,6]{2,1,0:T(1,128)} %bitcast.4), calls=%async_computation | async-start | bytes 32768 | tf_op jit(solution)/shard_map/all_to_all | solution.py:163
  19.2 8.9 %collective-permute-done.1 = bf16[548,8,128]{2,1,0:T(8,128)(2,1)S(1)} collective-permute-done((bf16[548,8,128]{2,1,0:T(8,128)(2,1)S(1)}, bf16[548,8,128]{2,1,0:T(8,128)(2,1)S(1)}, u32[]{:S(2)}, u32[]{:S(2)}) %collective-permute-start.1) | collective-permute-done | bytes 1122336 | tf_op jit(solution)/shard_map/ppermute | solution.py:36
  28.3 25.8 %collective-permute-done = bf16[548,8,128]{2,1,0:T(8,128)(2,1)S(1)} collective-permute-done((bf16[548,8,128]{2,1,0:T(8,128)(2,1)S(1)}, bf16[548,8,128]{2,1,0:T(8,128)(2,1)S(1)}, u32[]{:S(2)}, u32[]{:S(2)}) %collective-permute-start) | collective-permute-done | bytes 1122336 | tf_op jit(solution)/shard_map/ppermute | solution.py:36
  54.2 3.6 %bitcast_convert_fusion.2 = (bf16[548,8,128]{2,1,0:T(8,128)(2,1)S(1)}, f32[548,128,8]{1,2,0:T(8,128)S(1)}) fusion(f32[]{:T(128)S(6)} %sqrt.8, f32[548,8,128]{2,1,0:T(8,128)S(1)} %convert_element_type.89, f32[548,8,128]{2,1,0:T(8,128)S(1)} %copy-done, f32[548,8,128]{2,1,0:T(8,128)S(1)} %convert_element_type.88), kind=kOutput, calls=%fused_computation.21 | convolution fusion | flops 165541760 | bytes 10100740 | tf_op jit(solution)/shard_map/ij,cjk->cik/dot_general | solution.py:54
  58.5 1.6 collective-permute-start.3
  65.7 5.1 %collective-permute-done.3 = bf16[274,8,128]{2,1,0:T(8,128)(2,1)} collective-permute-done((bf16[274,8,128]{2,1,0:T(8,128)(2,1)S(1)}, bf16[274,8,128]{2,1,0:T(8,128)(2,1)}, u32[]{:S(2)}, u32[]{:S(2)}) %collective-permute-start.3) | collective-permute-done | bytes 561184 | tf_op jit(solution)/shard_map/ppermute | solution.py:60
  70.8 2.7 %collective-permute-done.2 = bf16[274,8,128]{2,1,0:T(8,128)(2,1)} collective-permute-done((bf16[274,8,128]{2,1,0:T(8,128)(2,1)S(1)}, bf16[274,8,128]{2,1,0:T(8,128)(2,1)}, u32[]{:S(2)}, u32[]{:S(2)}) %collective-permute-start.2) | collective-permute-done | bytes 561184 | tf_op jit(solution)/shard_map/ppermute | solution.py:59
  73.5 1.7 fusion.17
  75.2 1.7 convolution_add_fusion.1
  77.5 5.5 %bitcast_multiply_fusion = (f32[548,8,128]{2,1,0:T(8,128)}, f32[4384,128]{1,0:T(8,128)}) fusion(f32[548]{0:T(1024)S(1)} %copy-done.6, f32[2192,128]{1,0:T(8,128)S(1)} %get-tuple-element.20, f32[2192,128]{1,0:T(8,128)S(1)} %get-tuple-element.19, f32[256,128]{1,0:T(8,128)S(1)} %fusion.23, f32[548,128,8]{1,2,0:T(8,128)S(1)} %get-tuple-element.32), kind=kOutput, calls=%fused_computation.20 | convolution fusion | flops 863612928 | bytes 9048064 | tf_op jit(solution)/shard_map/dot_general | solution.py:69
  83.0 2.4 %reshape.215 = f32[548,1024]{1,0:T(8,128)S(1)} reshape(f32[4384,128]{1,0:T(8,128)} %get-tuple-element.34) | data formatting | bytes 4489216 | tf_op jit(solution)/shard_map/reshape | solution.py:72
  88.4 7.9 %all-to-all-start.1 = ((bf16[32,6,548]{2,1,0:T(8,128)(2,1)}), bf16[32,6,548]{2,1,0:T(8,128)(2,1)S(1)}, u32[]{:S(2)}, u32[]{:S(2)}) async-start(bf16[32,6,548]{2,1,0:T(8,128)(2,1)} %reshape.217), calls=%async_computation.1 | async-start | bytes 655360 | tf_op jit(solution)/shard_map/all_to_all | solution.py:180
  98.3 4.2 %collective-permute-start.9 = (s32[192]{0:T(256)S(1)}, s32[192]{0:T(256)S(1)}, u32[]{:S(2)}, u32[]{:S(2)}) collective-permute-start(s32[192]{0:T(256)S(1)} %reshape.212), channel_id=1, source_target_pairs={{8,0},{16,8},{24,16},{9,1},{17,9},{25,17},{10,2},{18,10},{26,18},{... | collective-permute-start | bytes 2312 | tf_op jit(solution)/shard_map/ppermute | solution.py:36
  102.6 3.8 %all-to-all-done.1 = bf16[32,6,548]{2,1,0:T(8,128)(2,1)S(1)} async-done(((bf16[32,6,548]{2,1,0:T(8,128)(2,1)}), bf16[32,6,548]{2,1,0:T(8,128)(2,1)S(1)}, u32[]{:S(2)}, u32[]{:S(2)}) %all-to-all-start.1) | async-done | bytes 210464 | tf_op jit(solution)/shard_map/all_to_all | solution.py:180
  106.6 1.4 gather_fusion.1
  108.0 16.9 %soundings.1 = (f32[96,256]{1,0:T(8,128)}, f32[96,548]{1,0:T(8,128)}) custom-call(bf16[150,96,548]{2,1,0:T(8,128)(2,1)} %bitcast.57, bf16[96,548]{1,0:T(8,128)(2,1)} %gather_fusion.1, f32[96,256]{1,0:T(8,128)} %pad.8.innov_ref, f32[1,150]{1,0:T(1,128)} %bitcast.70), custom_call_target="tpu_custom_call" | custom-call | tf_op jit(solution)/shard_map/soundings/pallas_call | solution.py:123
  124.9 1.5 scatter_custom_fusion.1
  127.2 4.4 %all-to-all-start.2 = ((bf16[32,6,548]{2,1,0:T(8,128)(2,1)}), bf16[32,6,548]{2,1,0:T(8,128)(2,1)S(1)}, u32[]{:S(2)}, u32[]{:S(2)}) async-start(bf16[32,6,548]{2,1,0:T(8,128)(2,1)} %reshape.220), calls=%async_computation.2 | async-start | bytes 655360 | tf_op jit(solution)/shard_map/all_to_all | solution.py:186
  131.6 1.6 collective-permute-start.10
  133.5 3.5 %collective-permute-done.10 = s32[3,192]{1,0:T(4,128)S(1)} collective-permute-done((s32[3,192]{1,0:T(4,128)S(1)}, s32[3,192]{1,0:T(4,128)S(1)}, u32[]{:S(2)}, u32[]{:S(2)}) %collective-permute-start.10) | collective-permute-done | bytes 2336 | tf_op jit(solution)/shard_map/ppermute | solution.py:36
  137.1 4.8 %all-to-all-done.2 = bf16[32,6,548]{2,1,0:T(8,128)(2,1)S(1)} async-done(((bf16[32,6,548]{2,1,0:T(8,128)(2,1)}), bf16[32,6,548]{2,1,0:T(8,128)(2,1)S(1)}, u32[]{:S(2)}, u32[]{:S(2)}) %all-to-all-start.2) | async-done | bytes 210464 | tf_op jit(solution)/shard_map/all_to_all | solution.py:186
  142.0 3.1 %collective-permute-start.5 = (bf16[192,548]{1,0:T(8,128)(2,1)S(1)}, bf16[192,548]{1,0:T(8,128)(2,1)S(1)}, u32[]{:S(2)}, u32[]{:S(2)}) collective-permute-start(bf16[192,548]{1,0:T(8,128)(2,1)S(1)} %reshape.221), channel_id=1, source_target_pairs={{8,0},{16,8},{24,16},{9,1},{17,9},{25,17},{10,2},{18,10},{26,18},{... | collective-permute-start | bytes 631304 | tf_op jit(solution)/shard_map/ppermute | solution.py:36
  146.9 3.5 %collective-permute-done.5 = bf16[192,548]{1,0:T(8,128)(2,1)S(1)} collective-permute-done((bf16[192,548]{1,0:T(8,128)(2,1)S(1)}, bf16[192,548]{1,0:T(8,128)(2,1)S(1)}, u32[]{:S(2)}, u32[]{:S(2)}) %collective-permute-start.5) | collective-permute-done | bytes 210464 | tf_op jit(solution)/shard_map/ppermute | solution.py:36
  150.4 7.3 %collective-permute-done.4 = bf16[192,548]{1,0:T(8,128)(2,1)S(1)} collective-permute-done((bf16[192,548]{1,0:T(8,128)(2,1)S(1)}, bf16[192,548]{1,0:T(8,128)(2,1)S(1)}, u32[]{:S(2)}, u32[]{:S(2)}) %collective-permute-start.4) | collective-permute-done | bytes 210464 | tf_op jit(solution)/shard_map/ppermute | solution.py:36
  160.9 7.6 %broadcast_multiply_fusion = f32[1728,8,128]{2,1,0:T(8,128)} fusion(f32[1728,128]{1,0:T(8,128)S(1)} %fusion.16, f32[1728,8]{1,0:T(8,128)S(1)} %copy.34), kind=kLoop, calls=%fused_computation.17 | loop fusion | flops 1769472 | bytes 8017920 | tf_op jit(solution)/shard_map/mul | solution.py:174
  170.5 7.0 %collective-permute-done.7 = bf16[576,548]{0,1:T(8,128)(2,1)S(1)} collective-permute-done((bf16[576,548]{0,1:T(8,128)(2,1)}, bf16[576,548]{0,1:T(8,128)(2,1)S(1)}, u32[]{:S(2)}, u32[]{:S(2)}) %collective-permute-start.7) | collective-permute-done | bytes 631328 | tf_op jit(solution)/shard_map/ppermute | solution.py:36
  178.4 5.0 %concatenate.48 = bf16[1728,548]{0,1:T(8,128)(2,1)} concatenate(bf16[192,548]{0,1:T(8,128)(2,1)S(1)} %copy.31, bf16[192,548]{0,1:T(8,128)(2,1)S(1)} %copy.32, bf16[192,548]{0,1:T(8,128)(2,1)} %copy.33, bf16[576,548]{0,1:T(8,128)(2,1)} %collective-permute-done.6, bf16[576,548]{0,1:T(8,128)(2,1)} %copy-done.2), dimensions={0} | concatenate | bytes 3787776 | tf_op jit(solution)/shard_map/concatenate | solution.py:190
  183.4 6.0 %fusion.8 = f32[548,1024]{1,0:T(8,128)S(1)} fusion(bf16[1728,548]{0,1:T(8,128)(2,1)} %concatenate.48, f32[216,8,8,128]{3,2,1,0:T(8,128)} %bitcast.59), kind=kOutput, calls=%fused_computation.16 | convolution fusion | flops 1946419200 | bytes 11216384 | tf_op jit(solution)/shard_map/dot_general | solution.py:191
  189.5 2.3 %add_multiply_fusion = f32[548,1024]{1,0:T(8,128)S(1)} fusion(f32[548,1024]{1,0:T(8,128)S(1)} %fusion.8, bf16[1728,548]{0,1:T(8,128)(2,1)S(1)} %copy-done.1, f32[216,8,8,128]{3,2,1,0:T(8,128)S(1)} %bitcast.62, f32[548]{0:T(1024)S(1)} %copy-done.6), kind=kOutput, calls=%fused_computation.18 | convolution fusion | flops 1940463616 | bytes 13463184 | tf_op jit(solution)/shard_map/dot_general | solution.py:191
  192.4 1.5 slice.59
  (94 shorter events, 26.6 us)
Async XLA Ops:
  0.6 5.3 %copy-start.12 = (s32[96,1]{0,1:T(1,128)S(1)}, s32[96,1]{0,1:T(1,128)}, u32[]{:S(2)}) copy-start(s32[96,1]{0,1:T(1,128)} %param.10) | copy-start | bytes 1156
  2.4 25.7 %collective-permute-start.1 = (bf16[548,8,128]{2,1,0:T(8,128)(2,1)S(1)}, bf16[548,8,128]{2,1,0:T(8,128)(2,1)S(1)}, u32[]{:S(2)}, u32[]{:S(2)}) collective-permute-start(bf16[548,8,128]{2,1,0:T(8,128)(2,1)S(1)} %convert_element_type.87), channel_id=1, source_target_pairs={{8,0},{16,8},{24,16},{9,1},{17,9},{25,17},{10,2},{18,10},{26,18},{... | collective-permute-start | bytes 3366920 | tf_op jit(solution)/shard_map/ppermute | solution.py:36
  4.6 49.4 %collective-permute-start = (bf16[548,8,128]{2,1,0:T(8,128)(2,1)S(1)}, bf16[548,8,128]{2,1,0:T(8,128)(2,1)S(1)}, u32[]{:S(2)}, u32[]{:S(2)}) collective-permute-start(bf16[548,8,128]{2,1,0:T(8,128)(2,1)S(1)} %convert_element_type.87), channel_id=1, source_target_pairs={{0,8},{8,16},{16,24},{1,9},{9,17},{17,25},{2,10},{10,18},{18,26},{... | collective-permute-start | bytes 3366920 | tf_op jit(solution)/shard_map/ppermute | solution.py:36
  6.1 12.3 %copy-start.10 = (s32[96]{0:T(128)}, s32[96]{0:T(128)S(1)}, u32[]{:S(2)}) copy-start(s32[96]{0:T(128)S(1)} %fusion.60) | copy-start | bytes 1156
  7.8 54.5 %all-to-all-start = ((s32[32,1,6]{2,1,0:T(1,128)}), s32[32,1,6]{2,1,0:T(1,128)S(1)}, u32[]{:S(2)}, u32[]{:S(2)}) async-start(s32[32,1,6]{2,1,0:T(1,128)} %bitcast.4), calls=%async_computation | async-start | bytes 32768 | tf_op jit(solution)/shard_map/all_to_all | solution.py:163
  28.2 25.9 %copy-start = (f32[548,8,128]{2,1,0:T(8,128)S(1)}, f32[548,8,128]{2,1,0:T(8,128)}, u32[]{:S(2)}) copy-start(f32[548,8,128]{2,1,0:T(8,128)} %param.8) | copy-start | bytes 6733828
  58.5 12.3 %collective-permute-start.3 = (bf16[274,8,128]{2,1,0:T(8,128)(2,1)S(1)}, bf16[274,8,128]{2,1,0:T(8,128)(2,1)}, u32[]{:S(2)}, u32[]{:S(2)}) collective-permute-start(bf16[274,8,128]{2,1,0:T(8,128)(2,1)S(1)} %pad_maximum_fusion.2), channel_id=1, source_target_pairs={{1,0},{2,1},{3,2},{4,3},{5,4},{6,5},{7,6},{0,7},{9,8},{10,9},{11,1... | collective-permute-start | bytes 1683464 | tf_op jit(solution)/shard_map/ppermute | solution.py:60
  60.5 13.0 %collective-permute-start.2 = (bf16[274,8,128]{2,1,0:T(8,128)(2,1)S(1)}, bf16[274,8,128]{2,1,0:T(8,128)(2,1)}, u32[]{:S(2)}, u32[]{:S(2)}) collective-permute-start(bf16[274,8,128]{2,1,0:T(8,128)(2,1)S(1)} %pad_maximum_fusion.1), channel_id=1, source_target_pairs={{0,1},{1,2},{2,3},{3,4},{4,5},{5,6},{6,7},{7,0},{8,9},{9,10},{10,1... | collective-permute-start | bytes 1683464 | tf_op jit(solution)/shard_map/ppermute | solution.py:59
  65.1 10.1 %copy-start.3 = (f32[64,128]{1,0:T(8,128)S(1)}, f32[64,128]{1,0:T(8,128)}, u32[]{:S(2)}) copy-start(f32[64,128]{1,0:T(8,128)} %get-tuple-element.26) | copy-start | bytes 98308
  76.9 0.7 copy-start.6
  85.6 1.8 copy-start.7
  86.4 9.9 %copy-start.5 = (f32[96,150]{0,1:T(8,128)S(1)}, f32[96,150]{0,1:T(8,128)}, u32[]{:S(2)}) copy-start(f32[96,150]{0,1:T(8,128)} %param.13) | copy-start | bytes 172804
  86.4 10.6 %copy-start.11 = (s32[96]{0:T(128)S(1)}, s32[96]{0:T(128)}, u32[]{:S(2)}) copy-start(s32[96]{0:T(128)} %copy-done.10) | copy-start | bytes 1156
  88.4 18.0 %all-to-all-start.1 = ((bf16[32,6,548]{2,1,0:T(8,128)(2,1)}), bf16[32,6,548]{2,1,0:T(8,128)(2,1)S(1)}, u32[]{:S(2)}, u32[]{:S(2)}) async-start(bf16[32,6,548]{2,1,0:T(8,128)(2,1)} %reshape.217), calls=%async_computation.1 | async-start | bytes 655360 | tf_op jit(solution)/shard_map/all_to_all | solution.py:180
  97.0 34.6 %collective-permute-start.8 = (s32[192]{0:T(256)S(1)}, s32[192]{0:T(256)S(1)}, u32[]{:S(2)}, u32[]{:S(2)}) collective-permute-start(s32[192]{0:T(256)S(1)} %reshape.212), channel_id=1, source_target_pairs={{0,8},{8,16},{16,24},{1,9},{9,17},{17,25},{2,10},{10,18},{18,26},{... | collective-permute-start | bytes 2312 | tf_op jit(solution)/shard_map/ppermute | solution.py:36
  98.3 33.3 %collective-permute-start.9 = (s32[192]{0:T(256)S(1)}, s32[192]{0:T(256)S(1)}, u32[]{:S(2)}, u32[]{:S(2)}) collective-permute-start(s32[192]{0:T(256)S(1)} %reshape.212), channel_id=1, source_target_pairs={{8,0},{16,8},{24,16},{9,1},{17,9},{25,17},{10,2},{18,10},{26,18},{... | collective-permute-start | bytes 2312 | tf_op jit(solution)/shard_map/ppermute | solution.py:36
  108.0 25.2 %copy-start.9 = (s32[3]{0:T(128)S(1)}, s32[3]{0:T(128)}, u32[]{:S(2)}) copy-start(s32[3]{0:T(128)} %constant.107) | copy-start | bytes 40
  108.0 25.3 %copy-start.8 = (s32[3]{0:T(128)S(1)}, s32[3]{0:T(128)}, u32[]{:S(2)}) copy-start(s32[3]{0:T(128)} %constant.108) | copy-start | bytes 40
  127.2 14.7 %all-to-all-start.2 = ((bf16[32,6,548]{2,1,0:T(8,128)(2,1)}), bf16[32,6,548]{2,1,0:T(8,128)(2,1)S(1)}, u32[]{:S(2)}, u32[]{:S(2)}) async-start(bf16[32,6,548]{2,1,0:T(8,128)(2,1)} %reshape.220), calls=%async_computation.2 | async-start | bytes 655360 | tf_op jit(solution)/shard_map/all_to_all | solution.py:186
  131.6 5.3 %collective-permute-start.10 = (s32[3,192]{1,0:T(4,128)S(1)}, s32[3,192]{1,0:T(4,128)S(1)}, u32[]{:S(2)}, u32[]{:S(2)}) collective-permute-start(s32[3,192]{1,0:T(4,128)S(1)} %get-tuple-element.30), channel_id=1, source_target_pairs={{0,1},{1,2},{2,3},{3,4},{4,5},{5,6},{6,7},{7,0},{8,9},{9,10},{10,1... | collective-permute-start | bytes 6920 | tf_op jit(solution)/shard_map/ppermute | solution.py:36
  133.2 3.8 %collective-permute-start.11 = (s32[3,192]{1,0:T(4,128)S(1)}, s32[3,192]{1,0:T(4,128)S(1)}, u32[]{:S(2)}, u32[]{:S(2)}) collective-permute-start(s32[3,192]{1,0:T(4,128)S(1)} %get-tuple-element.30), channel_id=1, source_target_pairs={{1,0},{2,1},{3,2},{4,3},{5,4},{6,5},{7,6},{0,7},{9,8},{10,9},{11,1... | collective-permute-start | bytes 6920 | tf_op jit(solution)/shard_map/ppermute | solution.py:36
  142.0 8.3 %collective-permute-start.5 = (bf16[192,548]{1,0:T(8,128)(2,1)S(1)}, bf16[192,548]{1,0:T(8,128)(2,1)S(1)}, u32[]{:S(2)}, u32[]{:S(2)}) collective-permute-start(bf16[192,548]{1,0:T(8,128)(2,1)S(1)} %reshape.221), channel_id=1, source_target_pairs={{8,0},{16,8},{24,16},{9,1},{17,9},{25,17},{10,2},{18,10},{26,18},{... | collective-permute-start | bytes 631304 | tf_op jit(solution)/shard_map/ppermute | solution.py:36
  145.2 12.5 %collective-permute-start.4 = (bf16[192,548]{1,0:T(8,128)(2,1)S(1)}, bf16[192,548]{1,0:T(8,128)(2,1)S(1)}, u32[]{:S(2)}, u32[]{:S(2)}) collective-permute-start(bf16[192,548]{1,0:T(8,128)(2,1)S(1)} %reshape.221), channel_id=1, source_target_pairs={{0,8},{8,16},{16,24},{1,9},{9,17},{17,25},{2,10},{10,18},{18,26},{... | collective-permute-start | bytes 631304 | tf_op jit(solution)/shard_map/ppermute | solution.py:36
  158.9 18.7 %collective-permute-start.7 = (bf16[576,548]{0,1:T(8,128)(2,1)}, bf16[576,548]{0,1:T(8,128)(2,1)S(1)}, u32[]{:S(2)}, u32[]{:S(2)}) collective-permute-start(bf16[576,548]{0,1:T(8,128)(2,1)} %copy.29), channel_id=1, source_target_pairs={{1,0},{2,1},{3,2},{4,3},{5,4},{6,5},{7,6},{0,7},{9,8},{10,9},{11,1... | collective-permute-start | bytes 1893896 | tf_op jit(solution)/shard_map/ppermute | solution.py:36
  159.2 19.2 %collective-permute-start.6 = (bf16[576,548]{0,1:T(8,128)(2,1)}, bf16[576,548]{0,1:T(8,128)(2,1)}, u32[]{:S(2)}, u32[]{:S(2)}) collective-permute-start(bf16[576,548]{0,1:T(8,128)(2,1)} %copy.29), channel_id=1, source_target_pairs={{0,1},{1,2},{2,3},{3,4},{4,5},{5,6},{6,7},{7,0},{8,9},{9,10},{10,1... | collective-permute-start | bytes 1893896 | tf_op jit(solution)/shard_map/ppermute | solution.py:36
  160.9 7.6 %copy-start.4 = (f32[96,256]{1,0:T(8,128)S(1)}, f32[96,256]{1,0:T(8,128)}, u32[]{:S(2)}) copy-start(f32[96,256]{1,0:T(8,128)} %get-tuple-element.5) | copy-start | bytes 294916
  177.5 0.9 copy-start.2
  178.4 11.0 %slice-start = ((s8[7077888]{0:T(1024)(128)(4,1)}), s8[2883584]{0:T(1024)(128)(4,1)S(1)}, s32[]{:S(2)}) async-start(s8[7077888]{0:T(1024)(128)(4,1)} %bitcast.60), calls=%async_computation.3 | async-start | bytes 5767168
  183.4 6.0 %slice-start.1 = ((s8[7077888]{0:T(1024)(128)(4,1)}), s8[4194304]{0:T(1024)(128)(4,1)S(1)}, s32[]{:S(2)}) async-start(s8[7077888]{0:T(1024)(128)(4,1)} %bitcast.60), calls=%async_computation.4 | async-start | bytes 8388608
  183.4 6.0 %copy-start.1 = (bf16[1728,548]{0,1:T(8,128)(2,1)S(1)}, bf16[1728,548]{0,1:T(8,128)(2,1)}, u32[]{:S(2)}) copy-start(bf16[1728,548]{0,1:T(8,128)(2,1)} %concatenate.48) | copy-start | bytes 5681668
where the time goes:
time: 195 us; the launch traced here: 194 us
  waiting for transfers between devices  72.3 us (37%)
  starting transfers between devices  40.4 us (21%)
  local copies, waits for them, and re-layouts  25 us (13%)
  matrix products  21 us (11%)
  Pallas kernels  16.9 us (9%)
  other arithmetic  15.8 us (8%)
  between operations  2.51 us (1%)
    ppermute x10, waiting for transfers between devices, around(): return (lax.ppermute(array, axis, up), lax.ppermute(array, axis, down))  55.9 us
    pallas_call x1, Pallas kernels, sounding_step(): pl.pallas_call(functools.partial(sounding_kernel, channels, step), grid=(...  16.9 us
    ppermute x10, starting transfers between devices, around(): return (lax.ppermute(array, axis, up), lax.ppermute(array, axis, down))  16.7 us
    all_to_all x1, starting transfers between devices, local(): lax.all_to_all(wanted.reshape(devices, slots_each), ('lat', 'lon'), split...  8.62 us
    dot_general x2, matrix products, local(): lax.dot_general(near, w, (((0,), (0,)), ((), ())), preferred_element_type...  8.36 us
    all_to_all x1, starting transfers between devices, local(): lax.all_to_all(picked.reshape(devices, slots_each, width), ('lat', 'lon')...  7.86 us
    mul x1, other arithmetic, local(): row_weight[:, :, None] * col_weight[:, None, :]  7.63 us
    dot_general x1, matrix products, smooth(): jnp.dot(field.reshape(width * lat_rows, lon_cols), lon_band[lon_half:-lon...  5.5 us
  transfers between devices with their start and end apart: 15, of which 10 were waited for; matrix products, arithmetic and copies ran while one was open for 14% of the time, Pallas kernels for 9%

commit v1 on v0

--- a/solution.py
+++ b/solution.py
@@ -9,6 +9,7 @@
 
 LHALF = 8
 HIGHEST = lax.Precision.HIGHEST
+MESH = pl.DeviceIdType.MESH
 
 
 def tap_weights(offset, half_width):
@@ -47,10 +48,13 @@
     return dot(high) + dot(low)
 
 
-def smooth(field, before, after):
+def smooth(field, swapped, far):
     width, lat_rows, lon_cols = field.shape
-    extended = jnp.concatenate([before.astype(jnp.float32), field, after.astype(jnp.float32)], axis=1)
+    extended = jnp.concatenate([swapped.astype(jnp.float32), field, far.astype(jnp.float32)], axis=1)
     lat_band = band(lat_rows, lat_rows + 2 * LHALF, LHALF)
+    before, middle, after = lat_band[:, :LHALF], lat_band[:, LHALF:-LHALF], lat_band[:, -LHALF:]
+    odd = lax.axis_index("lat") % 2 == 1
+    lat_band = jnp.concatenate([jnp.where(odd, before, after), middle, jnp.where(odd, after, before)], axis=1)
     field = jnp.einsum("ij,cjk->cik", lat_band, extended, precision=HIGHEST)
     lon_half, part = lon_cols // 2, width // 2
     rounded = field.astype(jnp.bfloat16)
@@ -70,6 +74,127 @@
         field.reshape(width * lat_rows, lon_cols), lon_band[lon_half:-lon_half], precision=HIGHEST
     )
     return (own + sides).reshape(width, lat_rows, lon_cols)
+
+
+def exchange_kernel(
+    lat, lon, cuts, tile_ref, wanted_ref, swap_ref, far_ref, requested_ref,
+    swap_send, swap_recv, far_send, far_recv, want_send, want_recv,
+):
+    row, column = lax.axis_index("lat"), lax.axis_index("lon")
+    devices, me = lat * lon, row * lon + column
+    odd = row % 2
+    partner, step = row + 1 - 2 * odd, 2 - 4 * odd
+    onward = jnp.logical_and(row + step >= 0, row + step < lat)
+    comes = jnp.logical_and(row - step >= 0, row - step < lat)
+    place = lambda other: (other // lon, other % lon)
+
+    barrier = pltpu.get_barrier_semaphore()
+
+    def greet(d, carry):
+        other = (me + d) % devices
+        pl.semaphore_signal(barrier, inc=1, device_id=place(other), device_id_type=MESH)
+        return carry
+
+    lax.fori_loop(1, devices, greet, 0)
+    pl.semaphore_wait(barrier, devices - 1)
+
+    def request(src, dst, send, recv, other):
+        return pltpu.make_async_remote_copy(
+            src_ref=wanted_ref.at[src],
+            dst_ref=requested_ref.at[dst],
+            send_sem=want_send.at[send],
+            recv_sem=want_recv.at[recv],
+            device_id=place(other),
+            device_id_type=MESH,
+        )
+
+    def ask(d, carry):
+        other = (me + d) % devices
+        request(other, me, other, me, other).start()
+        return carry
+
+    lax.fori_loop(1, devices, ask, 0)
+
+    def swap(k):
+        part = pl.ds(cuts[k], cuts[k + 1] - cuts[k])
+        return pltpu.make_async_remote_copy(
+            src_ref=tile_ref.at[part],
+            dst_ref=swap_ref.at[part],
+            send_sem=swap_send.at[k],
+            recv_sem=swap_recv.at[k],
+            device_id=(partner, column),
+            device_id_type=MESH,
+        )
+
+    def forward(k):
+        part = pl.ds(cuts[k], cuts[k + 1] - cuts[k])
+        return pltpu.make_async_remote_copy(
+            src_ref=swap_ref.at[part],
+            dst_ref=far_ref.at[part],
+            send_sem=far_send.at[k],
+            recv_sem=far_recv.at[k],
+            device_id=(row + step, column),
+            device_id_type=MESH,
+        )
+
+    pieces = range(len(cuts) - 1)
+    for k in pieces:
+        swap(k).start()
+    requested_ref[me] = wanted_ref[me]
+
+    @pl.when(jnp.logical_not(comes))
+    def _():
+        far_ref[...] = jnp.zeros_like(far_ref)
+
+    for k in pieces:
+        swap(k).wait_recv()
+
+        @pl.when(onward)
+        def _():
+            forward(k).start()
+
+    def hear(d, carry):
+        other = (me + d) % devices
+        asked = request(other, other, other, other, other)
+        asked.wait_send()
+        asked.wait_recv()
+        return carry
+
+    lax.fori_loop(1, devices, hear, 0)
+    for k in pieces:
+        swap(k).wait_send()
+
+        @pl.when(comes)
+        def _():
+            forward(k).wait_recv()
+
+        @pl.when(onward)
+        def _():
+            forward(k).wait_send()
+
+
+def exchange(tile, wanted):
+    lat, lon = lax.axis_size("lat"), lax.axis_size("lon")
+    devices, slots_each = wanted.shape
+    width, pieces = tile.shape[0], 6
+    cuts = [width * k // pieces for k in range(pieces + 1)]
+    wanted = jnp.pad(wanted, ((0, 0), (0, -slots_each % 128)))[:, None, :]
+    vmem = pl.BlockSpec(memory_space=pltpu.VMEM)
+    dma = pltpu.SemaphoreType.DMA
+    swapped, far, requested = pl.pallas_call(
+        functools.partial(exchange_kernel, lat, lon, cuts),
+        in_specs=[vmem, vmem],
+        out_specs=[vmem, vmem, vmem],
+        out_shape=[
+            jax.ShapeDtypeStruct(tile.shape, tile.dtype),
+            jax.ShapeDtypeStruct(tile.shape, tile.dtype),
+            jax.ShapeDtypeStruct(wanted.shape, wanted.dtype),
+        ],
+        scratch_shapes=[dma((pieces,))] * 4 + [dma((devices,))] * 2,
+        compiler_params=pltpu.CompilerParams(collective_id=0, has_side_effects=True),
+        name="exchange",
+    )(tile, wanted)
+    return swapped, far, requested[:, 0, :slots_each]
 
 
 def lane_tiles(count):
@@ -149,8 +274,6 @@
     slots_each = max(2, 2 * sound_count // devices)
     slots = devices * slots_each
 
-    before, after = around(control.astype(jnp.bfloat16), "lat", False)
-
     target = col_dev[:, 0]
     onehot = (target[:, None] == jnp.arange(devices, dtype=jnp.int32)[None, :]).astype(jnp.int32)
     below = jnp.arange(sound_count)[:, None] > jnp.arange(sound_count)[None, :]
@@ -160,9 +283,10 @@
     order_in = jnp.sum(earlier * onehot, axis=1)
     slot = target * slots_each + order_in
     wanted = jnp.zeros((slots,), jnp.int32).at[slot].set(col_cell)
-    requested = lax.all_to_all(
-        wanted.reshape(devices, slots_each), ("lat", "lon"), split_axis=0, concat_axis=0, tiled=True
-    ).reshape(-1)
+    swapped, far, requested = exchange(
+        control.astype(jnp.bfloat16), wanted.reshape(devices, slots_each)
+    )
+    requested = requested.reshape(-1)
 
     cells = jnp.stack([requested, *around(requested, "lat", False)])
     cells = jnp.stack([cells, *around(cells, "lon", True)]).reshape(3, 3, slots)
@@ -171,10 +295,10 @@
     columns_at = (cells % lon_cols + lon_cols * shift[:, None, None]).reshape(-1, 1)
     row_weight = tap_weights((rows - jnp.arange(lat_rows)[None, :]).astype(jnp.float32), LHALF)
     col_weight = tap_weights((columns_at - jnp.arange(lon_cols)[None, :]).astype(jnp.float32), lon_cols // 2)
-    spread = (row_weight[:, :, None] * col_weight[:, None, :]).reshape(-1, lat_rows * lon_cols)
+    spread = (row_weight[:, :, None] * col_weight[:, None, :]).reshape(3, 3 * slots, lat_rows * lon_cols)
     spread_high, spread_low = halves(spread)
 
-    increment = smooth(control, before, after) * std_dev[:, None, None]
+    increment = smooth(control, swapped, far) * std_dev[:, None, None]
     flat_field = increment.reshape(width, lat_rows * lon_cols)
     picked = jnp.take(flat_field, requested, axis=1).T.astype(jnp.bfloat16)
     returned = lax.all_to_all(
@@ -187,11 +311,13 @@
         outgoing.reshape(devices, slots_each, width), ("lat", "lon"), split_axis=0, concat_axis=0, tiled=True
     ).reshape(slots, width)
     near = jnp.concatenate([arrived, *around(arrived, "lat", False)], axis=0)
-    near = jnp.concatenate([near, *around(near, "lon", True)], axis=0)
-    add_up = lambda w: lax.dot_general(
-        near, w, (((0,), (0,)), ((), ())), preferred_element_type=jnp.float32
-    )
-    adjoint = (add_up(spread_high) + add_up(spread_low)) * std_dev[:, None]
+    adjoint = jnp.zeros((width, lat_rows * lon_cols), jnp.float32)
+    for at, grads in enumerate([near, *around(near, "lon", True)]):
+        for spread in (spread_high, spread_low):
+            adjoint += lax.dot_general(
+                grads, spread[at], (((0,), (0,)), ((), ())), preferred_element_type=jnp.float32
+            )
+    adjoint = adjoint * std_dev[:, None]
     return (departures, increment, adjoint.reshape(width, lat_rows, lon_cols))
 
 

time: 195 us -> 207 us (1.062)
  the two profiles are of different devices: /device:TPU:7 before, /device:TPU:0 now
where the time goes in v1:
time: 207 us; the launch traced here: 205 us
  Pallas kernels  57.3 us (28%)
  local copies, waits for them, and re-layouts  37.9 us (18%)
  waiting for transfers between devices  33.3 us (16%)
  other arithmetic  27.7 us (13%)
  starting transfers between devices  25 us (12%)
  matrix products  21.7 us (10%)
  between operations  2.49 us (1%)
    pallas_call x1, Pallas kernels, exchange(): pl.pallas_call(functools.partial(exchange_kernel, lat, lon, cuts), in_spe...  40.4 us
    ppermute x8, waiting for transfers between devices, around(): return (lax.ppermute(array, axis, up), lax.ppermute(array, axis, down))  21.7 us
    ppermute x8, starting transfers between devices, around(): return (lax.ppermute(array, axis, up), lax.ppermute(array, axis, down))  17 us
    pallas_call x1, Pallas kernels, sounding_step(): pl.pallas_call(functools.partial(sounding_kernel, channels, step), grid=(...  16.9 us
    all_to_all x1, waiting for transfers between devices, local(): lax.all_to_all(picked.reshape(devices, slots_each, width), ('lat', 'lon')...  11.6 us
    convert_element_type x1, other arithmetic, halves(): return (high, (weights - high.astype(jnp.float32)).astype(jnp.bfloat16))  9.16 us
    dot_general x6, matrix products, local(): lax.dot_general(grads, spread[at], (((0,), (0,)), ((), ())), preferred_el...  9.14 us
    unnamed x31, local copies, waits for them, and re-layouts  9.04 us
  transfers between devices with their start and end apart: 12, of which 5 were waited for; matrix products, arithmetic and copies ran while one was open for 26% of the time, Pallas kernels for 0%

profile of v1, /device:TPU:0, one launch (start us, length us, event | category | flops | bytes accessed | tf_op | source)
XLA Modules:
  0.0 205.5 jit_solution(2042687720217264644)
XLA Ops:
  0.6 2.7 %convert_element_type.84.tile_ref = bf16[548,8,128]{2,1,0:T(8,128)(2,1)} convert(f32[548,8,128]{2,1,0:T(8,128)} %param.8) | non-fusion elementwise | flops 561152 | bytes 3366912 | tf_op jit(solution)/shard_map/convert_element_type | solution.py:287
  5.3 40.4 %exchange.1 = (bf16[548,8,128]{2,1,0:T(8,128)(2,1)}, bf16[548,8,128]{2,1,0:T(8,128)(2,1)}, s32[32,1,128]{2,1,0:T(1,128)}) custom-call(bf16[548,8,128]{2,1,0:T(8,128)(2,1)} %convert_element_type.84.tile_ref, s32[32,1,128]{2,1,0:T(1,128)} %bitcast.73), custom_call_target="tpu_custom_call" | custom-call | tf_op jit(solution)/shard_map/exchange/pallas_call | solution.py:184
  48.0 5.0 %collective-permute-start.4 = (s32[192]{0:T(256)S(1)}, s32[192]{0:T(256)S(1)}, u32[]{:S(2)}, u32[]{:S(2)}) collective-permute-start(s32[192]{0:T(256)S(1)} %reshape_squeeze.5), channel_id=1, source_target_pairs={{0,8},{8,16},{16,24},{1,9},{9,17},{17,25},{2,10},{10,18},{18,26},{... | collective-permute-start | bytes 2312 | tf_op jit(solution)/shard_map/ppermute | solution.py:37
  57.4 3.5 %bitcast_convert_fusion = (bf16[548,8,128]{2,1,0:T(8,128)(2,1)S(1)}, f32[548,128,8]{1,2,0:T(8,128)S(1)}) fusion(f32[8,8]{1,0:T(8,128)S(1)} %get-tuple-element.41, f32[8,8]{1,0:T(8,128)S(1)} %get-tuple-element.40, f32[8,8]{1,0:T(8,128)S(1)} %get-tuple-element.39, f32[548,8,128]{2,1,0:T(8,128)S(1)} %convert_element_type.89, f32[548,8,128]{2,1,0:T(8,128)S(1)} %copy-done, ...), kind=kOutput, calls=%fused_computation.17 | convolution fusion | flops 165540224 | bytes 10101504 | tf_op jit(solution)/shard_map/ij,cjk->cik/dot_general | solution.py:58
  66.1 3.1 %collective-permute-start.7 = (s32[3,192]{1,0:T(4,128)S(1)}, s32[3,192]{1,0:T(4,128)S(1)}, u32[]{:S(2)}, u32[]{:S(2)}) collective-permute-start(s32[3,192]{1,0:T(4,128)S(1)} %get-tuple-element.43), channel_id=1, source_target_pairs={{1,0},{2,1},{3,2},{4,3},{5,4},{6,5},{7,6},{0,7},{9,8},{10,9},{11,1... | collective-permute-start | bytes 6920 | tf_op jit(solution)/shard_map/ppermute | solution.py:37
  69.8 1.6 copy.23
  71.7 1.5 pad.13.innov_ref
  74.6 1.6 collective-permute-done.6
  78.2 1.7 fusion.19
  79.9 1.7 convolution_add_fusion.1
  82.3 5.5 %bitcast_multiply_fusion = (f32[548,8,128]{2,1,0:T(8,128)}, f32[4384,128]{1,0:T(8,128)}) fusion(f32[548]{0:T(1024)S(1)} %copy-done.6, f32[2192,128]{1,0:T(8,128)S(1)} %get-tuple-element.28, f32[2192,128]{1,0:T(8,128)S(1)} %get-tuple-element.27, f32[256,128]{1,0:T(8,128)S(1)} %fusion.25, f32[548,128,8]{1,2,0:T(8,128)S(1)} %get-tuple-element.45), kind=kOutput, calls=%fused_computation.16 | convolution fusion | flops 863612928 | bytes 9048064 | tf_op jit(solution)/shard_map/dot_general | solution.py:73
  87.8 2.4 %reshape.205 = f32[548,1024]{1,0:T(8,128)S(1)} reshape(f32[4384,128]{1,0:T(8,128)} %get-tuple-element.47) | data formatting | bytes 4489216 | tf_op jit(solution)/shard_map/reshape | solution.py:76
  93.4 4.8 %all-to-all-start = ((bf16[32,6,548]{2,1,0:T(8,128)(2,1)}), bf16[32,6,548]{2,1,0:T(8,128)(2,1)S(1)}, u32[]{:S(2)}, u32[]{:S(2)}) async-start(bf16[32,6,548]{2,1,0:T(8,128)(2,1)} %reshape.206), calls=%async_computation | async-start | bytes 655360 | tf_op jit(solution)/shard_map/all_to_all | solution.py:304
  98.6 11.6 %all-to-all-done = bf16[32,6,548]{2,1,0:T(8,128)(2,1)S(1)} async-done(((bf16[32,6,548]{2,1,0:T(8,128)(2,1)}), bf16[32,6,548]{2,1,0:T(8,128)(2,1)S(1)}, u32[]{:S(2)}, u32[]{:S(2)}) %all-to-all-start) | async-done | bytes 210464 | tf_op jit(solution)/shard_map/all_to_all | solution.py:304
  110.4 1.6 gather_fusion.1
  111.9 16.9 %soundings.1 = (f32[96,256]{1,0:T(8,128)}, f32[96,548]{1,0:T(8,128)}) custom-call(bf16[150,96,548]{2,1,0:T(8,128)(2,1)} %bitcast.67, bf16[96,548]{1,0:T(8,128)(2,1)} %gather_fusion.1, f32[96,256]{1,0:T(8,128)} %pad.13.innov_ref, f32[1,150]{1,0:T(1,128)} %bitcast.77), custom_call_target="tpu_custom_call" | custom-call | tf_op jit(solution)/shard_map/soundings/pallas_call | solution.py:248
  128.8 1.5 scatter_custom_fusion.1
  131.2 2.6 %all-to-all-start.1 = ((bf16[32,6,548]{2,1,0:T(8,128)(2,1)}), bf16[32,6,548]{2,1,0:T(8,128)(2,1)S(1)}, u32[]{:S(2)}, u32[]{:S(2)}) async-start(bf16[32,6,548]{2,1,0:T(8,128)(2,1)} %reshape.209), calls=%async_computation.1 | async-start | bytes 655360 | tf_op jit(solution)/shard_map/all_to_all | solution.py:310
  133.8 7.6 %broadcast_multiply_fusion = f32[1728,8,128]{2,1,0:T(8,128)} fusion(f32[1728,128]{1,0:T(8,128)S(1)} %fusion.18, f32[1728,8]{1,0:T(8,128)S(1)} %copy-done.2), kind=kLoop, calls=%fused_computation.13 | loop fusion | flops 1769472 | bytes 8017920 | tf_op jit(solution)/shard_map/mul | solution.py:298
  141.4 8.6 %mul.101 = f32[3,576,1024]{2,1,0:T(8,128)} reshape(f32[1728,8,128]{2,1,0:T(8,128)} %broadcast_multiply_fusion) | data formatting | bytes 14155776 | tf_op jit(solution)/shard_map/mul | solution.py:298
  150.8 4.3 %collective-permute-start.2 = (bf16[192,548]{1,0:T(8,128)(2,1)}, bf16[192,548]{1,0:T(8,128)(2,1)}, u32[]{:S(2)}, u32[]{:S(2)}) collective-permute-start(bf16[192,548]{1,0:T(8,128)(2,1)} %reshape.210), channel_id=1, source_target_pairs={{0,8},{8,16},{16,24},{1,9},{9,17},{17,25},{2,10},{10,18},{18,26},{... | collective-permute-start | bytes 631304 | tf_op jit(solution)/shard_map/ppermute | solution.py:37
  155.1 9.2 %subtract_convert_fusion = (bf16[3,576,1024]{2,1,0:T(8,128)(2,1)S(1)}, bf16[3,576,1024]{2,1,0:T(8,128)(2,1)}) fusion(f32[3,576,1024]{2,1,0:T(8,128)} %mul.101), kind=kLoop, calls=%fused_computation.4 | loop fusion | flops 7077888 | bytes 14155776 | tf_op jit(solution)/shard_map/convert_element_type | solution.py:42
  164.2 1.6 copy.27
  167.2 1.7 constant_dynamic-update-slice_fusion.2
  168.8 1.7 constant_dynamic-update-slice_fusion.1
  170.5 5.2 %collective-permute-done.3 = bf16[192,548]{1,0:T(8,128)(2,1)S(1)} collective-permute-done((bf16[192,548]{1,0:T(8,128)(2,1)}, bf16[192,548]{1,0:T(8,128)(2,1)S(1)}, u32[]{:S(2)}, u32[]{:S(2)}) %collective-permute-start.3) | collective-permute-done | bytes 210464 | tf_op jit(solution)/shard_map/ppermute | solution.py:37
  176.4 2.3 %copy.25 = bf16[576,548]{0,1:T(8,128)(2,1)} copy(bf16[576,548]{1,0:T(8,128)(2,1)} %constant_dynamic-update-slice_fusion) | data formatting | bytes 1262592 | tf_op jit(solution)/shard_map/concatenate | solution.py:313
  178.6 2.1 collective-permute-start.9
  180.7 2.6 %fusion.12 = f32[548,1024]{1,0:T(8,128)S(1)} fusion(bf16[576,548]{1,0:T(8,128)(2,1)} %constant_dynamic-update-slice_fusion, bf16[3,576,1024]{2,1,0:T(8,128)(2,1)} %get-tuple-element.26), kind=kOutput, calls=%fused_computation.30 | convolution fusion | flops 646447104 | bytes 4161536 | tf_op jit(solution)/shard_map/dot_general | solution.py:317
  183.3 2.2 %fusion.11 = f32[548,1024]{1,0:T(8,128)S(1)} fusion(bf16[576,548]{1,0:T(8,128)(2,1)} %constant_dynamic-update-slice_fusion, bf16[3,576,1024]{2,1,0:T(8,128)(2,1)S(1)} %get-tuple-element.25), kind=kOutput, calls=%fused_computation.28 | convolution fusion | flops 646447104 | bytes 4055552 | tf_op jit(solution)/shard_map/dot_general | solution.py:317
  185.5 13.5 %collective-permute-done.8 = bf16[576,548]{0,1:T(8,128)(2,1)S(1)} collective-permute-done((bf16[576,548]{0,1:T(8,128)(2,1)}, bf16[576,548]{0,1:T(8,128)(2,1)S(1)}, u32[]{:S(2)}, u32[]{:S(2)}) %collective-permute-start.8) | collective-permute-done | bytes 631328 | tf_op jit(solution)/shard_map/ppermute | solution.py:37
  203.9 1.5 slice.105
  (90 shorter events, 29.2 us)
Async XLA Ops:
  0.6 2.8 %copy-start.12 = (s32[96,1]{0,1:T(1,128)S(1)}, s32[96,1]{0,1:T(1,128)}, u32[]{:S(2)}) copy-start(s32[96,1]{0,1:T(1,128)} %param.10) | copy-start | bytes 1156
  3.6 61.8 %copy-start.9 = (s32[96]{0:T(128)}, s32[96]{0:T(128)S(1)}, u32[]{:S(2)}) copy-start(s32[96]{0:T(128)S(1)} %fusion.55) | copy-start | bytes 1156
  45.7 10.1 %copy-start.3 = (bf16[548,8,128]{2,1,0:T(8,128)(2,1)S(1)}, bf16[548,8,128]{2,1,0:T(8,128)(2,1)}, u32[]{:S(2)}) copy-start(bf16[548,8,128]{2,1,0:T(8,128)(2,1)} %get-tuple-element.9) | copy-start | bytes 3366916
  46.7 19.3 %collective-permute-start.5 = (s32[192]{0:T(256)S(1)}, s32[192]{0:T(256)S(1)}, u32[]{:S(2)}, u32[]{:S(2)}) collective-permute-start(s32[192]{0:T(256)S(1)} %reshape_squeeze.5), channel_id=1, source_target_pairs={{8,0},{16,8},{24,16},{9,1},{17,9},{25,17},{10,2},{18,10},{26,18},{... | collective-permute-start | bytes 2312 | tf_op jit(solution)/shard_map/ppermute | solution.py:37
  48.0 18.0 %collective-permute-start.4 = (s32[192]{0:T(256)S(1)}, s32[192]{0:T(256)S(1)}, u32[]{:S(2)}, u32[]{:S(2)}) collective-permute-start(s32[192]{0:T(256)S(1)} %reshape_squeeze.5), channel_id=1, source_target_pairs={{0,8},{8,16},{16,24},{1,9},{9,17},{17,25},{2,10},{10,18},{18,26},{... | collective-permute-start | bytes 2312 | tf_op jit(solution)/shard_map/ppermute | solution.py:37
  55.8 1.6 copy-start
  61.4 10.0 %copy-start.11 = (s32[3]{0:T(128)S(1)}, s32[3]{0:T(128)}, u32[]{:S(2)}) copy-start(s32[3]{0:T(128)} %constant.126) | copy-start | bytes 40
  61.4 10.1 %copy-start.10 = (s32[3]{0:T(128)S(1)}, s32[3]{0:T(128)}, u32[]{:S(2)}) copy-start(s32[3]{0:T(128)} %constant.127) | copy-start | bytes 40
  61.7 16.4 %collective-permute-start.1 = (bf16[274,8,128]{2,1,0:T(8,128)(2,1)S(1)}, bf16[274,8,128]{2,1,0:T(8,128)(2,1)}, u32[]{:S(2)}, u32[]{:S(2)}) collective-permute-start(bf16[274,8,128]{2,1,0:T(8,128)(2,1)S(1)} %pad_maximum_fusion.1), channel_id=1, source_target_pairs={{1,0},{2,1},{3,2},{4,3},{5,4},{6,5},{7,6},{0,7},{9,8},{10,9},{11,1... | collective-permute-start | bytes 1683464 | tf_op jit(solution)/shard_map/ppermute | solution.py:64
  62.1 16.1 %collective-permute-start = (bf16[274,8,128]{2,1,0:T(8,128)(2,1)S(1)}, bf16[274,8,128]{2,1,0:T(8,128)(2,1)}, u32[]{:S(2)}, u32[]{:S(2)}) collective-permute-start(bf16[274,8,128]{2,1,0:T(8,128)(2,1)S(1)} %pad_maximum_fusion), channel_id=1, source_target_pairs={{0,1},{1,2},{2,3},{3,4},{4,5},{5,6},{6,7},{7,0},{8,9},{9,10},{10,1... | collective-permute-start | bytes 1683464 | tf_op jit(solution)/shard_map/ppermute | solution.py:63
  66.1 8.5 %collective-permute-start.7 = (s32[3,192]{1,0:T(4,128)S(1)}, s32[3,192]{1,0:T(4,128)S(1)}, u32[]{:S(2)}, u32[]{:S(2)}) collective-permute-start(s32[3,192]{1,0:T(4,128)S(1)} %get-tuple-element.43), channel_id=1, source_target_pairs={{1,0},{2,1},{3,2},{4,3},{5,4},{6,5},{7,6},{0,7},{9,8},{10,9},{11,1... | collective-permute-start | bytes 6920 | tf_op jit(solution)/shard_map/ppermute | solution.py:37
  69.2 7.0 %collective-permute-start.6 = (s32[3,192]{1,0:T(4,128)S(1)}, s32[3,192]{1,0:T(4,128)S(1)}, u32[]{:S(2)}, u32[]{:S(2)}) collective-permute-start(s32[3,192]{1,0:T(4,128)S(1)} %get-tuple-element.43), channel_id=1, source_target_pairs={{0,1},{1,2},{2,3},{3,4},{4,5},{5,6},{6,7},{7,0},{8,9},{9,10},{10,1... | collective-permute-start | bytes 6920 | tf_op jit(solution)/shard_map/ppermute | solution.py:37
  78.2 1.7 copy-start.4
  78.2 1.7 copy-start.5
  81.6 0.7 copy-start.6
  90.4 2.1 copy-start.8
  91.1 7.1 %copy-start.7 = (s32[1728]{0:T(1024)S(1)}, s32[1728]{0:T(1024)}, u32[]{:S(2)}) copy-start(s32[1728]{0:T(1024)} %get-tuple-element.38) | copy-start | bytes 20740
  93.4 16.8 %all-to-all-start = ((bf16[32,6,548]{2,1,0:T(8,128)(2,1)}), bf16[32,6,548]{2,1,0:T(8,128)(2,1)S(1)}, u32[]{:S(2)}, u32[]{:S(2)}) async-start(bf16[32,6,548]{2,1,0:T(8,128)(2,1)} %reshape.206), calls=%async_computation | async-start | bytes 655360 | tf_op jit(solution)/shard_map/all_to_all | solution.py:304
  128.8 5.0 %copy-start.2 = (f32[1728,8]{1,0:T(8,128)S(1)}, f32[1728,8]{1,0:T(8,128)}, u32[]{:S(2)}) copy-start(f32[1728,8]{1,0:T(8,128)} %copy.24) | copy-start | bytes 165892
  131.2 18.8 %all-to-all-start.1 = ((bf16[32,6,548]{2,1,0:T(8,128)(2,1)}), bf16[32,6,548]{2,1,0:T(8,128)(2,1)S(1)}, u32[]{:S(2)}, u32[]{:S(2)}) async-start(bf16[32,6,548]{2,1,0:T(8,128)(2,1)} %reshape.209), calls=%async_computation.1 | async-start | bytes 655360 | tf_op jit(solution)/shard_map/all_to_all | solution.py:310
  150.8 18.0 %collective-permute-start.2 = (bf16[192,548]{1,0:T(8,128)(2,1)}, bf16[192,548]{1,0:T(8,128)(2,1)}, u32[]{:S(2)}, u32[]{:S(2)}) collective-permute-start(bf16[192,548]{1,0:T(8,128)(2,1)} %reshape.210), channel_id=1, source_target_pairs={{0,8},{8,16},{16,24},{1,9},{9,17},{17,25},{2,10},{10,18},{18,26},{... | collective-permute-start | bytes 631304 | tf_op jit(solution)/shard_map/ppermute | solution.py:37
  165.9 9.8 %collective-permute-start.3 = (bf16[192,548]{1,0:T(8,128)(2,1)}, bf16[192,548]{1,0:T(8,128)(2,1)S(1)}, u32[]{:S(2)}, u32[]{:S(2)}) collective-permute-start(bf16[192,548]{1,0:T(8,128)(2,1)} %reshape.210), channel_id=1, source_target_pairs={{8,0},{16,8},{24,16},{9,1},{17,9},{25,17},{10,2},{18,10},{26,18},{... | collective-permute-start | bytes 631304 | tf_op jit(solution)/shard_map/ppermute | solution.py:37
  178.6 22.5 %collective-permute-start.9 = (bf16[576,548]{0,1:T(8,128)(2,1)}, bf16[576,548]{0,1:T(8,128)(2,1)S(1)}, u32[]{:S(2)}, u32[]{:S(2)}) collective-permute-start(bf16[576,548]{0,1:T(8,128)(2,1)} %copy.25), channel_id=1, source_target_pairs={{1,0},{2,1},{3,2},{4,3},{5,4},{6,5},{7,6},{0,7},{9,8},{10,9},{11,1... | collective-permute-start | bytes 1893896 | tf_op jit(solution)/shard_map/ppermute | solution.py:37
  180.7 18.3 %collective-permute-start.8 = (bf16[576,548]{0,1:T(8,128)(2,1)}, bf16[576,548]{0,1:T(8,128)(2,1)S(1)}, u32[]{:S(2)}, u32[]{:S(2)}) collective-permute-start(bf16[576,548]{0,1:T(8,128)(2,1)} %copy.25), channel_id=1, source_target_pairs={{0,1},{1,2},{2,3},{3,4},{4,5},{5,6},{6,7},{7,0},{8,9},{9,10},{10,1... | collective-permute-start | bytes 1893896 | tf_op jit(solution)/shard_map/ppermute | solution.py:37
  185.5 14.6 %copy-start.1 = (bf16[3,576,1024]{2,1,0:T(8,128)(2,1)S(1)}, bf16[3,576,1024]{2,1,0:T(8,128)(2,1)}, u32[]{:S(2)}) copy-start(bf16[3,576,1024]{2,1,0:T(8,128)(2,1)} %get-tuple-element.26) | copy-start | bytes 10616836

commit v2 on v1

--- a/solution.py
+++ b/solution.py
@@ -98,9 +98,9 @@
     lax.fori_loop(1, devices, greet, 0)
     pl.semaphore_wait(barrier, devices - 1)
 
-    def request(src, dst, send, recv, other):
+    def request(dst, send, recv, other):
         return pltpu.make_async_remote_copy(
-            src_ref=wanted_ref.at[src],
+            src_ref=wanted_ref.at[0],
             dst_ref=requested_ref.at[dst],
             send_sem=want_send.at[send],
             recv_sem=want_recv.at[recv],
@@ -110,7 +110,7 @@
 
     def ask(d, carry):
         other = (me + d) % devices
-        request(other, me, other, me, other).start()
+        request(me, other, me, other).start()
         return carry
 
     lax.fori_loop(1, devices, ask, 0)
@@ -140,7 +140,7 @@
     pieces = range(len(cuts) - 1)
     for k in pieces:
         swap(k).start()
-    requested_ref[me] = wanted_ref[me]
+    requested_ref[me] = wanted_ref[0]
 
     @pl.when(jnp.logical_not(comes))
     def _():
@@ -155,7 +155,7 @@
 
     def hear(d, carry):
         other = (me + d) % devices
-        asked = request(other, other, other, other, other)
+        asked = request(other, other, other, other)
         asked.wait_send()
         asked.wait_recv()
         return carry
@@ -175,10 +175,10 @@
 
 def exchange(tile, wanted):
     lat, lon = lax.axis_size("lat"), lax.axis_size("lon")
-    devices, slots_each = wanted.shape
+    devices, slots = lat * lon, wanted.shape[0]
     width, pieces = tile.shape[0], 6
     cuts = [width * k // pieces for k in range(pieces + 1)]
-    wanted = jnp.pad(wanted, ((0, 0), (0, -slots_each % 128)))[:, None, :]
+    wanted = jnp.pad(wanted, (0, -slots % 128))[None, None, :]
     vmem = pl.BlockSpec(memory_space=pltpu.VMEM)
     dma = pltpu.SemaphoreType.DMA
     swapped, far, requested = pl.pallas_call(
@@ -188,13 +188,13 @@
         out_shape=[
             jax.ShapeDtypeStruct(tile.shape, tile.dtype),
             jax.ShapeDtypeStruct(tile.shape, tile.dtype),
-            jax.ShapeDtypeStruct(wanted.shape, wanted.dtype),
+            jax.ShapeDtypeStruct((devices, *wanted.shape[1:]), wanted.dtype),
         ],
         scratch_shapes=[dma((pieces,))] * 4 + [dma((devices,))] * 2,
         compiler_params=pltpu.CompilerParams(collective_id=0, has_side_effects=True),
         name="exchange",
     )(tile, wanted)
-    return swapped, far, requested[:, 0, :slots_each]
+    return swapped, far, requested[:, 0, :slots]
 
 
 def lane_tiles(count):
@@ -267,6 +267,41 @@
     return departures[:, :channels], grad
 
 
+def adjoint_kernel(near_ref, before_ref, after_ref, col_ref, row_ref, std_ref, out_ref):
+    lon_cols = col_ref.shape[1]
+    total = jnp.zeros((2 * lon_cols, near_ref.shape[1]), jnp.float32)
+    for at, grads in enumerate((near_ref, before_ref, after_ref)):
+        high, low = halves(col_ref[at] * row_ref[0, at])
+        both = jnp.concatenate([high, low], axis=0)
+        total = total + jnp.dot(both, grads[...], preferred_element_type=jnp.float32)
+    total = (total[:lon_cols] + total[lon_cols:]) * std_ref[...]
+    out_ref[...] = total.T
+
+
+def adjoint_step(grads, rows, columns_at, std_dev, lat_rows, lon_cols):
+    slots, width = grads[0].shape
+    down = jnp.arange(lat_rows)[:, None, None, None]
+    row_weight = tap_weights((rows[None, :, None, :] - down).astype(jnp.float32), LHALF)
+    along = jnp.arange(lon_cols)[None, :, None]
+    col_weight = tap_weights((columns_at[:, None, :] - along).astype(jnp.float32), lon_cols // 2)
+    whole = pl.BlockSpec((slots, width), lambda i: (0, 0))
+    return pl.pallas_call(
+        adjoint_kernel,
+        grid=(lat_rows,),
+        in_specs=[
+            whole,
+            whole,
+            whole,
+            pl.BlockSpec((3, lon_cols, slots), lambda i: (0, 0, 0)),
+            pl.BlockSpec((1, 3, 1, slots), lambda i: (i, 0, 0, 0)),
+            pl.BlockSpec((1, width), lambda i: (0, 0)),
+        ],
+        out_specs=pl.BlockSpec((width, lon_cols), lambda i: (0, i)),
+        out_shape=jax.ShapeDtypeStruct((width, lat_rows * lon_cols), jnp.float32),
+        name="adjoint",
+    )(*grads, col_weight, row_weight, std_dev[None, :])
+
+
 def local(control, std_dev, col_dev, col_cell, jacobian, innovation, inv_error):
     width, lat_rows, lon_cols = control.shape
     devices = lax.axis_size("lat") * lax.axis_size("lon")
@@ -283,20 +318,16 @@
     order_in = jnp.sum(earlier * onehot, axis=1)
     slot = target * slots_each + order_in
     wanted = jnp.zeros((slots,), jnp.int32).at[slot].set(col_cell)
-    swapped, far, requested = exchange(
-        control.astype(jnp.bfloat16), wanted.reshape(devices, slots_each)
-    )
-    requested = requested.reshape(-1)
-
-    cells = jnp.stack([requested, *around(requested, "lat", False)])
-    cells = jnp.stack([cells, *around(cells, "lon", True)]).reshape(3, 3, slots)
-    shift = jnp.array([0, -1, 1], jnp.int32)
-    rows = (cells // lon_cols + lat_rows * shift[None, :, None]).reshape(-1, 1)
-    columns_at = (cells % lon_cols + lon_cols * shift[:, None, None]).reshape(-1, 1)
-    row_weight = tap_weights((rows - jnp.arange(lat_rows)[None, :]).astype(jnp.float32), LHALF)
-    col_weight = tap_weights((columns_at - jnp.arange(lon_cols)[None, :]).astype(jnp.float32), lon_cols // 2)
-    spread = (row_weight[:, :, None] * col_weight[:, None, :]).reshape(3, 3 * slots, lat_rows * lon_cols)
-    spread_high, spread_low = halves(spread)
+    swapped, far, table = exchange(control.astype(jnp.bfloat16), wanted)
+    lat_at, lon_at = lax.axis_index("lat"), lax.axis_index("lon")
+    lat_devices, lon_devices = lax.axis_size("lat"), lax.axis_size("lon")
+
+    def asked_of(lat_shift, lon_shift):
+        row = jnp.clip(lat_at + lat_shift, 0, lat_devices - 1)
+        owner = row * lon_devices + (lon_at + lon_shift) % lon_devices
+        return lax.dynamic_slice(table, (0, owner * slots_each), (devices, slots_each))
+
+    requested = asked_of(0, 0).reshape(-1)
 
     increment = smooth(control, swapped, far) * std_dev[:, None, None]
     flat_field = increment.reshape(width, lat_rows * lon_cols)
@@ -311,13 +342,14 @@
         outgoing.reshape(devices, slots_each, width), ("lat", "lon"), split_axis=0, concat_axis=0, tiled=True
     ).reshape(slots, width)
     near = jnp.concatenate([arrived, *around(arrived, "lat", False)], axis=0)
-    adjoint = jnp.zeros((width, lat_rows * lon_cols), jnp.float32)
-    for at, grads in enumerate([near, *around(near, "lon", True)]):
-        for spread in (spread_high, spread_low):
-            adjoint += lax.dot_general(
-                grads, spread[at], (((0,), (0,)), ((), ())), preferred_element_type=jnp.float32
-            )
-    adjoint = adjoint * std_dev[:, None]
+    grads = (near, *around(near, "lon", True))
+    order = (0, -1, 1)
+    cells = jnp.stack([jnp.stack([asked_of(up, along) for up in order]) for along in order])
+    cells = cells.reshape(3, 3, slots)
+    shift = jnp.array(order, jnp.int32)
+    rows = (cells // lon_cols + lat_rows * shift[None, :, None]).reshape(3, 3 * slots)
+    columns_at = (cells % lon_cols + lon_cols * shift[:, None, None]).reshape(3, 3 * slots)
+    adjoint = adjoint_step(grads, rows, columns_at, std_dev, lat_rows, lon_cols)
     return (departures, increment, adjoint.reshape(width, lat_rows, lon_cols))
 
 

time: 207 us -> 189 us (0.913)
  waiting for transfers between devices: 33.3 us -> 54.4 us
  other arithmetic: 27.7 us -> 10.4 us
  local copies, waits for them, and re-layouts: 37.9 us -> 25.5 us
  Pallas kernels: 57.3 us -> 68.8 us
  starting transfers between devices: 25 us -> 14.1 us
  matrix products: 21.7 us -> 12.5 us
    pallas_call x0 -> x1, Pallas kernels: none -> 11.3 us  [adjoint_step(): pl.pallas_call(adjoint_kernel, grid=(lat_rows,), in_specs=[whole, whole,...]
    ppermute x8 -> x4, starting transfers between devices: 17 us -> 6.57 us  [around(): return (lax.ppermute(array, axis, up), lax.ppermute(array, axis, down))]
    all_to_all x1, waiting for transfers between devices: 0.01 us -> 10.1 us  [local(): lax.all_to_all(outgoing.reshape(devices, slots_each, width), ('lat', 'lon...]
    convert_element_type x2 -> x1, other arithmetic: 11.9 us -> 2.74 us  [local(): swapped, far, table = exchange(control.astype(jnp.bfloat16), wanted)]
    dot_general x6 -> x0, matrix products: 9.14 us -> none  [local(): lax.dot_general(grads, spread[at], (((0,), (0,)), ((), ())), preferred_el...]
    mul x1 -> x0, local copies, waits for them, and re-layouts: 8.56 us -> none  [local(): row_weight[:, :, None] * col_weight[:, None, :]]
    mul x1 -> x0, other arithmetic: 7.64 us -> none  [local(): row_weight[:, :, None] * col_weight[:, None, :]]
    ppermute x1, waiting for transfers between devices: 0.01 us -> 6.46 us  [smooth(): right = lax.ppermute(paired(rounded[:, :, :lon_half]), 'lon', down)]
  transfers between devices with their start and end apart: 12 -> 8, of which waited for: 5 -> 7; matrix products, arithmetic and copies ran while one was open for 26% -> 6% of each run, Pallas kernels for 0% -> 0%
where the time goes in v2:
time: 189 us; the launch traced here: 188 us
  Pallas kernels  68.8 us (36%)
  waiting for transfers between devices  54.4 us (29%)
  local copies, waits for them, and re-layouts  25.5 us (13%)
  starting transfers between devices  14.1 us (7%)
  matrix products  12.5 us (7%)
  other arithmetic  10.4 us (6%)
  between operations  2.53 us (1%)
    pallas_call x1, Pallas kernels, exchange(): pl.pallas_call(functools.partial(exchange_kernel, lat, lon, cuts), in_spe...  40.6 us
    ppermute x4, waiting for transfers between devices, around(): return (lax.ppermute(array, axis, up), lax.ppermute(array, axis, down))  24.6 us
    pallas_call x1, Pallas kernels, sounding_step(): pl.pallas_call(functools.partial(sounding_kernel, channels, step), grid=(...  17 us
    all_to_all x1, waiting for transfers between devices, local(): lax.all_to_all(picked.reshape(devices, slots_each, width), ('lat', 'lon')...  11.3 us
    pallas_call x1, Pallas kernels, adjoint_step(): pl.pallas_call(adjoint_kernel, grid=(lat_rows,), in_specs=[whole, whole,...  11.3 us
    all_to_all x1, waiting for transfers between devices, local(): lax.all_to_all(outgoing.reshape(devices, slots_each, width), ('lat', 'lon...  10.1 us
    ppermute x4, starting transfers between devices, around(): return (lax.ppermute(array, axis, up), lax.ppermute(array, axis, down))  6.57 us
    ppermute x1, waiting for transfers between devices, smooth(): right = lax.ppermute(paired(rounded[:, :, :lon_half]), 'lon', down)  6.46 us
  transfers between devices with their start and end apart: 8, of which 7 were waited for; matrix products, arithmetic and copies ran while one was open for 6% of the time, Pallas kernels for 0%

profile of v2, /device:TPU:0, one launch (start us, length us, event | category | flops | bytes accessed | tf_op | source)
XLA Modules:
  0.0 188.3 jit_solution(4825604338842591212)
XLA Ops:
  2.0 2.7 %convert_element_type.75.tile_ref = bf16[548,8,128]{2,1,0:T(8,128)(2,1)} convert(f32[548,8,128]{2,1,0:T(8,128)} %param.8) | non-fusion elementwise | flops 561152 | bytes 3366912 | tf_op jit(solution)/shard_map/convert_element_type | solution.py:321
  6.5 40.6 %exchange.1 = (bf16[548,8,128]{2,1,0:T(8,128)(2,1)}, bf16[548,8,128]{2,1,0:T(8,128)(2,1)}, s32[32,1,256]{2,1,0:T(1,128)}) custom-call(bf16[548,8,128]{2,1,0:T(8,128)(2,1)} %convert_element_type.75.tile_ref, s32[1,1,256]{2,1,0:T(1,128)} %bitcast.60), custom_call_target="tpu_custom_call" | custom-call | tf_op jit(solution)/shard_map/exchange/pallas_call | solution.py:184
  47.1 1.5 convert_element_type.80
  48.9 1.4 copy-done
  50.3 3.5 %bitcast_convert_fusion = (bf16[548,8,128]{2,1,0:T(8,128)(2,1)S(1)}, f32[548,128,8]{1,2,0:T(8,128)S(1)}) fusion(f32[8,8]{1,0:T(8,128)S(1)} %get-tuple-element.55, f32[8,8]{1,0:T(8,128)S(1)} %get-tuple-element.54, f32[8,8]{1,0:T(8,128)S(1)} %get-tuple-element.53, f32[548,8,128]{2,1,0:T(8,128)S(1)} %convert_element_type.80, f32[548,8,128]{2,1,0:T(8,128)S(1)} %copy-done, ...), kind=kOutput, calls=%fused_computation.14 | convolution fusion | flops 165540224 | bytes 10101504 | tf_op jit(solution)/shard_map/ij,cjk->cik/dot_general | solution.py:58
  57.4 2.3 %constant_dynamic-slice_fusion.7 = (s32[32,1,6]{2,1,0:T(1,128)}, s32[32,1,6]{2,1,0:T(1,128)}, s32[32,1,6]{2,1,0:T(1,128)}, s32[32,1,6]{2,1,0:T(1,128)}, s32[32,1...) fusion(s32[32,1,192]{2,1,0:T(1,128)S(1)} %bitcast.48, ...), kind=kLoop, calls=%fused_computation.103 | loop fusion | bytes 14632 | tf_op jit(solution)/shard_map/dynamic_slice | solution.py:328
  60.7 6.5 %collective-permute-done.1 = bf16[274,8,128]{2,1,0:T(8,128)(2,1)} collective-permute-done((bf16[274,8,128]{2,1,0:T(8,128)(2,1)S(1)}, bf16[274,8,128]{2,1,0:T(8,128)(2,1)}, u32[]{:S(2)}, u32[]{:S(2)}) %collective-permute-start.1) | collective-permute-done | bytes 561184 | tf_op jit(solution)/shard_map/ppermute | solution.py:64
  67.2 1.9 %collective-permute-done = bf16[274,8,128]{2,1,0:T(8,128)(2,1)} collective-permute-done((bf16[274,8,128]{2,1,0:T(8,128)(2,1)S(1)}, bf16[274,8,128]{2,1,0:T(8,128)(2,1)}, u32[]{:S(2)}, u32[]{:S(2)}) %collective-permute-start) | collective-permute-done | bytes 561184 | tf_op jit(solution)/shard_map/ppermute | solution.py:63
  69.1 1.7 fusion.13
  70.8 1.7 convolution_add_fusion.1
  73.2 5.5 %bitcast_multiply_fusion = (f32[548,8,128]{2,1,0:T(8,128)}, f32[4384,128]{1,0:T(8,128)}) fusion(f32[548]{0:T(1024)S(1)} %copy-done.14, f32[2192,128]{1,0:T(8,128)S(1)} %get-tuple-element.34, f32[2192,128]{1,0:T(8,128)S(1)} %get-tuple-element.33, f32[256,128]{1,0:T(8,128)S(1)} %fusion.19, f32[548,128,8]{1,2,0:T(8,128)S(1)} %get-tuple-element.57), kind=kOutput, calls=%fused_computation.13 | convolution fusion | flops 863612928 | bytes 9048064 | tf_op jit(solution)/shard_map/dot_general | solution.py:73
  78.6 2.4 %reshape.334 = f32[548,1024]{1,0:T(8,128)S(1)} reshape(f32[4384,128]{1,0:T(8,128)} %get-tuple-element.59) | data formatting | bytes 4489216 | tf_op jit(solution)/shard_map/reshape | solution.py:76
  82.0 1.0 gather_fusion
  84.0 4.2 %all-to-all-start = ((bf16[32,6,548]{2,1,0:T(8,128)(2,1)}), bf16[32,6,548]{2,1,0:T(8,128)(2,1)S(1)}, u32[]{:S(2)}, u32[]{:S(2)}) async-start(bf16[32,6,548]{2,1,0:T(8,128)(2,1)} %reshape.336), calls=%async_computation | async-start | bytes 655360 | tf_op jit(solution)/shard_map/all_to_all | solution.py:335
  88.9 11.3 %all-to-all-done = bf16[32,6,548]{2,1,0:T(8,128)(2,1)S(1)} async-done(((bf16[32,6,548]{2,1,0:T(8,128)(2,1)}), bf16[32,6,548]{2,1,0:T(8,128)(2,1)S(1)}, u32[]{:S(2)}, u32[]{:S(2)}) %all-to-all-start) | async-done | bytes 210464 | tf_op jit(solution)/shard_map/all_to_all | solution.py:335
  100.3 1.4 gather_fusion.1
  101.8 17.0 %soundings.1 = (f32[96,256]{1,0:T(8,128)}, f32[96,548]{1,0:T(8,128)}) custom-call(bf16[150,96,548]{2,1,0:T(8,128)(2,1)} %bitcast.45, bf16[96,548]{1,0:T(8,128)(2,1)} %gather_fusion.1, f32[96,256]{1,0:T(8,128)} %pad.13.innov_ref, f32[1,150]{1,0:T(1,128)} %bitcast.62), custom_call_target="tpu_custom_call" | custom-call | tf_op jit(solution)/shard_map/soundings/pallas_call | solution.py:248
  118.8 1.5 scatter_custom_fusion.1
  121.1 2.7 %all-to-all-start.1 = ((bf16[32,6,548]{2,1,0:T(8,128)(2,1)}), bf16[32,6,548]{2,1,0:T(8,128)(2,1)S(1)}, u32[]{:S(2)}, u32[]{:S(2)}) async-start(bf16[32,6,548]{2,1,0:T(8,128)(2,1)} %reshape.339), calls=%async_computation.1 | async-start | bytes 655360 | tf_op jit(solution)/shard_map/all_to_all | solution.py:341
  125.7 10.1 %all-to-all-done.1 = bf16[32,6,548]{2,1,0:T(8,128)(2,1)S(1)} async-done(((bf16[32,6,548]{2,1,0:T(8,128)(2,1)}), bf16[32,6,548]{2,1,0:T(8,128)(2,1)S(1)}, u32[]{:S(2)}, u32[]{:S(2)}) %all-to-all-start.1) | async-done | bytes 210464 | tf_op jit(solution)/shard_map/all_to_all | solution.py:341
  136.0 1.7 collective-permute-start.2
  138.1 1.3 collective-permute-start.3
  139.4 4.4 %collective-permute-done.2 = bf16[192,548]{1,0:T(8,128)(2,1)S(1)} collective-permute-done((bf16[192,548]{1,0:T(8,128)(2,1)S(1)}, bf16[192,548]{1,0:T(8,128)(2,1)S(1)}, u32[]{:S(2)}, u32[]{:S(2)}) %collective-permute-start.2) | collective-permute-done | bytes 210464 | tf_op jit(solution)/shard_map/ppermute | solution.py:37
  143.8 7.6 %collective-permute-done.3 = bf16[192,548]{1,0:T(8,128)(2,1)S(1)} collective-permute-done((bf16[192,548]{1,0:T(8,128)(2,1)S(1)}, bf16[192,548]{1,0:T(8,128)(2,1)S(1)}, u32[]{:S(2)}, u32[]{:S(2)}) %collective-permute-start.3) | collective-permute-done | bytes 210464 | tf_op jit(solution)/shard_map/ppermute | solution.py:37
  151.8 3.5 %collective-permute-start.5 = (bf16[576,548]{0,1:T(8,128)(2,1)S(1)}, bf16[576,548]{0,1:T(8,128)(2,1)S(1)}, u32[]{:S(2)}, u32[]{:S(2)}) collective-permute-start(bf16[576,548]{0,1:T(8,128)(2,1)S(1)} %copy.76), channel_id=1, source_target_pairs={{1,0},{2,1},{3,2},{4,3},{5,4},{6,5},{7,6},{0,7},{9,8},{10,9},{11,1... | collective-permute-start | bytes 1893896 | tf_op jit(solution)/shard_map/ppermute | solution.py:37
  156.2 1.3 fusion.12.col_ref
  158.3 12.7 %collective-permute-done.4 = bf16[576,548]{0,1:T(8,128)(2,1)S(1)} collective-permute-done((bf16[576,548]{0,1:T(8,128)(2,1)S(1)}, bf16[576,548]{0,1:T(8,128)(2,1)S(1)}, u32[]{:S(2)}, u32[]{:S(2)}) %collective-permute-start.4) | collective-permute-done | bytes 631328 | tf_op jit(solution)/shard_map/ppermute | solution.py:37
  171.0 1.2 copy.90.before_ref
  172.2 1.2 copy.91.after_ref
  173.4 11.3 %adjoint.1 = f32[548,1024]{1,0:T(8,128)} custom-call(bf16[576,548]{1,0:T(8,128)(2,1)} %copy-done.1, bf16[576,548]{1,0:T(8,128)(2,1)} %copy.90.before_ref, bf16[576,548]{1,0:T(8,128)(2,1)} %copy.91.after_ref, f32[3,128,576]{2,1,0:T(8,128)} %fusion.12.col_ref, f32[8,3,1,576]{3,2,1,0:T(1,128)} %compare_select_fusion.row_ref, f32[1,548]{1,0:T(1,128)} %broadcast_in_dim.65.std_ref), custom_call_target="tpu_custom_call" | custom-call | tf_op jit(solution)/shard_map/adjoint/pallas_call | solution.py:288
  184.7 2.1 %copy.93 = f32[69,8,8,128]{3,2,1,0:T(8,128)S(1)} copy(f32[69,8,8,128]{3,1,2,0:T(8,128)} %bitcast.46) | data formatting | bytes 4521984
  186.8 1.5 slice.75
  (102 shorter events, 15.2 us)
Async XLA Ops:
  0.6 4.1 %copy-start.19 = (s32[96,1]{0,1:T(1,128)S(1)}, s32[96,1]{0,1:T(1,128)}, u32[]{:S(2)}) copy-start(s32[96,1]{0,1:T(1,128)} %param.10) | copy-start | bytes 1156
  4.9 43.7 %copy-start.17 = (s32[96]{0:T(128)}, s32[96]{0:T(128)S(1)}, u32[]{:S(2)}) copy-start(s32[96]{0:T(128)S(1)} %fusion.46) | copy-start | bytes 1156
  47.1 1.6 copy-start.2
  48.6 1.7 copy-start
  54.2 3.2 %copy-start.3 = (s32[32,1,256]{2,1,0:T(1,128)S(1)}, s32[32,1,256]{2,1,0:T(1,128)}, u32[]{:S(2)}) copy-start(s32[32,1,256]{2,1,0:T(1,128)} %get-tuple-element.8) | copy-start | bytes 98308
  54.6 12.6 %collective-permute-start.1 = (bf16[274,8,128]{2,1,0:T(8,128)(2,1)S(1)}, bf16[274,8,128]{2,1,0:T(8,128)(2,1)}, u32[]{:S(2)}, u32[]{:S(2)}) collective-permute-start(bf16[274,8,128]{2,1,0:T(8,128)(2,1)S(1)} %pad_maximum_fusion.1), channel_id=1, source_target_pairs={{1,0},{2,1},{3,2},{4,3},{5,4},{6,5},{7,6},{0,7},{9,8},{10,9},{11,1... | collective-permute-start | bytes 1683464 | tf_op jit(solution)/shard_map/ppermute | solution.py:64
  54.9 14.1 %collective-permute-start = (bf16[274,8,128]{2,1,0:T(8,128)(2,1)S(1)}, bf16[274,8,128]{2,1,0:T(8,128)(2,1)}, u32[]{:S(2)}, u32[]{:S(2)}) collective-permute-start(bf16[274,8,128]{2,1,0:T(8,128)(2,1)S(1)} %pad_maximum_fusion), channel_id=1, source_target_pairs={{0,1},{1,2},{2,3},{3,4},{4,5},{5,6},{6,7},{7,0},{8,9},{9,10},{10,1... | collective-permute-start | bytes 1683464 | tf_op jit(solution)/shard_map/ppermute | solution.py:63
  72.5 0.7 copy-start.14
  82.0 6.2 %copy-start.5 = (f32[96,150]{0,1:T(8,128)S(1)}, f32[96,150]{0,1:T(8,128)}, u32[]{:S(2)}) copy-start(f32[96,150]{0,1:T(8,128)} %param.13) | copy-start | bytes 172804
  82.0 6.9 %copy-start.18 = (s32[96]{0:T(128)S(1)}, s32[96]{0:T(128)}, u32[]{:S(2)}) copy-start(s32[96]{0:T(128)} %copy-done.17) | copy-start | bytes 1156
  84.0 16.2 %all-to-all-start = ((bf16[32,6,548]{2,1,0:T(8,128)(2,1)}), bf16[32,6,548]{2,1,0:T(8,128)(2,1)S(1)}, u32[]{:S(2)}, u32[]{:S(2)}) async-start(bf16[32,6,548]{2,1,0:T(8,128)(2,1)} %reshape.336), calls=%async_computation | async-start | bytes 655360 | tf_op jit(solution)/shard_map/all_to_all | solution.py:335
  101.8 22.7 %copy-start.13 = (s32[32,1,6]{2,1,0:T(1,128)S(1)}, s32[32,1,6]{2,1,0:T(1,128)}, u32[]{:S(2)}) copy-start(s32[32,1,6]{2,1,0:T(1,128)} %get-tuple-element.42) | copy-start | bytes 2308
  101.8 22.8 %copy-start.12 = (s32[32,1,6]{2,1,0:T(1,128)S(1)}, s32[32,1,6]{2,1,0:T(1,128)}, u32[]{:S(2)}) copy-start(s32[32,1,6]{2,1,0:T(1,128)} %get-tuple-element.43) | copy-start | bytes 2308
  101.8 22.8 %copy-start.11 = (s32[32,1,6]{2,1,0:T(1,128)S(1)}, s32[32,1,6]{2,1,0:T(1,128)}, u32[]{:S(2)}) copy-start(s32[32,1,6]{2,1,0:T(1,128)} %get-tuple-element.44) | copy-start | bytes 2308
  101.8 23.2 %copy-start.10 = (s32[32,1,6]{2,1,0:T(1,128)S(1)}, s32[32,1,6]{2,1,0:T(1,128)}, u32[]{:S(2)}) copy-start(s32[32,1,6]{2,1,0:T(1,128)} %get-tuple-element.45) | copy-start | bytes 2308
  101.8 23.3 %copy-start.9 = (s32[32,1,6]{2,1,0:T(1,128)S(1)}, s32[32,1,6]{2,1,0:T(1,128)}, u32[]{:S(2)}) copy-start(s32[32,1,6]{2,1,0:T(1,128)} %get-tuple-element.46) | copy-start | bytes 2308
  101.8 23.4 %copy-start.8 = (s32[32,1,6]{2,1,0:T(1,128)S(1)}, s32[32,1,6]{2,1,0:T(1,128)}, u32[]{:S(2)}) copy-start(s32[32,1,6]{2,1,0:T(1,128)} %get-tuple-element.47) | copy-start | bytes 2308
  101.8 23.7 %copy-start.7 = (s32[32,1,6]{2,1,0:T(1,128)S(1)}, s32[32,1,6]{2,1,0:T(1,128)}, u32[]{:S(2)}) copy-start(s32[32,1,6]{2,1,0:T(1,128)} %get-tuple-element.48) | copy-start | bytes 2308
  101.8 23.8 %copy-start.6 = (s32[32,1,6]{2,1,0:T(1,128)S(1)}, s32[32,1,6]{2,1,0:T(1,128)}, u32[]{:S(2)}) copy-start(s32[32,1,6]{2,1,0:T(1,128)} %get-tuple-element.41) | copy-start | bytes 2308
  118.8 19.2 %copy-start.16 = (s32[3]{0:T(128)S(1)}, s32[3]{0:T(128)}, u32[]{:S(2)}) copy-start(s32[3]{0:T(128)} %constant.174) | copy-start | bytes 40
  121.1 34.3 %copy-start.15 = (s32[3]{0:T(128)S(1)}, s32[3]{0:T(128)}, u32[]{:S(2)}) copy-start(s32[3]{0:T(128)} %constant.173) | copy-start | bytes 40
  121.1 14.8 %all-to-all-start.1 = ((bf16[32,6,548]{2,1,0:T(8,128)(2,1)}), bf16[32,6,548]{2,1,0:T(8,128)(2,1)S(1)}, u32[]{:S(2)}, u32[]{:S(2)}) async-start(bf16[32,6,548]{2,1,0:T(8,128)(2,1)} %reshape.339), calls=%async_computation.1 | async-start | bytes 655360 | tf_op jit(solution)/shard_map/all_to_all | solution.py:341
  125.7 31.9 %copy-start.4 = (f32[96,256]{1,0:T(8,128)S(1)}, f32[96,256]{1,0:T(8,128)}, u32[]{:S(2)}) copy-start(f32[96,256]{1,0:T(8,128)} %get-tuple-element.11) | copy-start | bytes 294916
  136.0 7.8 %collective-permute-start.2 = (bf16[192,548]{1,0:T(8,128)(2,1)S(1)}, bf16[192,548]{1,0:T(8,128)(2,1)S(1)}, u32[]{:S(2)}, u32[]{:S(2)}) collective-permute-start(bf16[192,548]{1,0:T(8,128)(2,1)S(1)} %reshape.340), channel_id=1, source_target_pairs={{0,8},{8,16},{16,24},{1,9},{9,17},{17,25},{2,10},{10,18},{18,26},{... | collective-permute-start | bytes 631304 | tf_op jit(solution)/shard_map/ppermute | solution.py:37
  138.1 13.3 %collective-permute-start.3 = (bf16[192,548]{1,0:T(8,128)(2,1)S(1)}, bf16[192,548]{1,0:T(8,128)(2,1)S(1)}, u32[]{:S(2)}, u32[]{:S(2)}) collective-permute-start(bf16[192,548]{1,0:T(8,128)(2,1)S(1)} %reshape.340), channel_id=1, source_target_pairs={{8,0},{16,8},{24,16},{9,1},{17,9},{25,17},{10,2},{18,10},{26,18},{... | collective-permute-start | bytes 631304 | tf_op jit(solution)/shard_map/ppermute | solution.py:37
  151.4 22.0 %copy-start.1 = (bf16[576,548]{1,0:T(8,128)(2,1)}, bf16[576,548]{1,0:T(8,128)(2,1)S(1)}, u32[]{:S(2)}) copy-start(bf16[576,548]{1,0:T(8,128)(2,1)S(1)} %constant_dynamic-update-slice_fusion.near_ref) | copy-start | bytes 1893892
  151.8 19.2 %collective-permute-start.4 = (bf16[576,548]{0,1:T(8,128)(2,1)S(1)}, bf16[576,548]{0,1:T(8,128)(2,1)S(1)}, u32[]{:S(2)}, u32[]{:S(2)}) collective-permute-start(bf16[576,548]{0,1:T(8,128)(2,1)S(1)} %copy.76), channel_id=1, source_target_pairs={{0,1},{1,2},{2,3},{3,4},{4,5},{5,6},{6,7},{7,0},{8,9},{9,10},{10,1... | collective-permute-start | bytes 1893896 | tf_op jit(solution)/shard_map/ppermute | solution.py:37
  151.8 20.4 %collective-permute-start.5 = (bf16[576,548]{0,1:T(8,128)(2,1)S(1)}, bf16[576,548]{0,1:T(8,128)(2,1)S(1)}, u32[]{:S(2)}, u32[]{:S(2)}) collective-permute-start(bf16[576,548]{0,1:T(8,128)(2,1)S(1)} %copy.76), channel_id=1, source_target_pairs={{1,0},{2,1},{3,2},{4,3},{5,4},{6,5},{7,6},{0,7},{9,8},{10,9},{11,1... | collective-permute-start | bytes 1893896 | tf_op jit(solution)/shard_map/ppermute | solution.py:37

commit v3 on v2

--- a/solution.py
+++ b/solution.py
@@ -201,17 +201,10 @@
     return -(-count // 128)
 
 
-def fold_lanes(tile):
-    rows, count = tile.shape
-    total = tile[:, :128]
-    for start in range(128, count, 128):
-        total = total + tile[:, start : start + 128]
-    return total
-
-
-def sounding_kernel(channels, step, jac_ref, col_ref, innov_ref, inv_ref, dep_ref, grad_ref):
+def sounding_kernel(channels, step, jac_ref, col_ref, innov_ref, inv_ref, dep_ref, out_ref, grad_ref):
     rows, width = col_ref.shape
-    lanes = lax.broadcasted_iota(jnp.int32, (rows, dep_ref.shape[1]), 1)
+    padded = dep_ref.shape[1]
+    lanes = lax.broadcasted_iota(jnp.int32, (rows, padded), 1)
     columns = col_ref[...].astype(jnp.float32)
     dep_ref[...] = jnp.zeros_like(dep_ref)
     grad_ref[...] = jnp.zeros_like(grad_ref)
@@ -222,10 +215,9 @@
         for k in range(step):
             channel = index * step + k
             product = jac_ref[channel].astype(jnp.float32) * columns
+            observed = jnp.where(lanes == channel, innov_ref[...], 0.0)
+            product = jnp.concatenate([product[:, :padded] - observed, product[:, padded:]], axis=1)
             departure = jnp.sum(product, axis=1, keepdims=True)
-            departure = departure - jnp.sum(
-                jnp.where(lanes == channel, innov_ref[...], 0.0), axis=1, keepdims=True
-            )
             found = found + jnp.where(lanes == channel, departure, 0.0)
             weight = (departure * inv_ref[0, channel]).astype(jnp.bfloat16)
             weighted.append(weight.astype(jnp.float32))
@@ -237,6 +229,8 @@
         return carry
 
     lax.fori_loop(0, channels // step, some, 0)
+    out_ref[...] = jnp.zeros_like(out_ref)
+    out_ref[:, :width] = grad_ref[...].astype(out_ref.dtype)
 
 
 def sounding_step(jacobian, columns, innovation, inv_error):
@@ -256,12 +250,13 @@
         ],
         out_specs=[
             pl.BlockSpec((rows, padded), lambda i: (i, 0)),
-            pl.BlockSpec((rows, width), lambda i: (i, 0)),
+            pl.BlockSpec((rows, lane_tiles(width) * 128), lambda i: (i, 0)),
         ],
         out_shape=[
             jax.ShapeDtypeStruct((count, padded), jnp.float32),
-            jax.ShapeDtypeStruct((count, width), jnp.float32),
-        ],
+            jax.ShapeDtypeStruct((count, lane_tiles(width) * 128), jnp.bfloat16),
+        ],
+        scratch_shapes=[pltpu.VMEM((rows, width), jnp.float32)],
         name="soundings",
     )(jnp.transpose(jacobian, (1, 0, 2)), columns, innovation, inv_error[None, :])
     return departures[:, :channels], grad
@@ -275,16 +270,18 @@
         both = jnp.concatenate([high, low], axis=0)
         total = total + jnp.dot(both, grads[...], preferred_element_type=jnp.float32)
     total = (total[:lon_cols] + total[lon_cols:]) * std_ref[...]
-    out_ref[...] = total.T
+    out_ref[...] = total.T[: out_ref.shape[0]]
 
 
 def adjoint_step(grads, rows, columns_at, std_dev, lat_rows, lon_cols):
-    slots, width = grads[0].shape
+    slots, wide = grads[0].shape
+    width = std_dev.shape[0]
+    std_dev = jnp.pad(std_dev, (0, wide - width))
     down = jnp.arange(lat_rows)[:, None, None, None]
     row_weight = tap_weights((rows[None, :, None, :] - down).astype(jnp.float32), LHALF)
     along = jnp.arange(lon_cols)[None, :, None]
     col_weight = tap_weights((columns_at[:, None, :] - along).astype(jnp.float32), lon_cols // 2)
-    whole = pl.BlockSpec((slots, width), lambda i: (0, 0))
+    whole = pl.BlockSpec((slots, wide), lambda i: (0, 0))
     return pl.pallas_call(
         adjoint_kernel,
         grid=(lat_rows,),
@@ -294,7 +291,7 @@
             whole,
             pl.BlockSpec((3, lon_cols, slots), lambda i: (0, 0, 0)),
             pl.BlockSpec((1, 3, 1, slots), lambda i: (i, 0, 0, 0)),
-            pl.BlockSpec((1, width), lambda i: (0, 0)),
+            pl.BlockSpec((1, wide), lambda i: (0, 0)),
         ],
         out_specs=pl.BlockSpec((width, lon_cols), lambda i: (0, i)),
         out_shape=jax.ShapeDtypeStruct((width, lat_rows * lon_cols), jnp.float32),
@@ -337,10 +334,11 @@
     )
     columns = returned.reshape(slots, width)[slot]
     departures, column_grad = sounding_step(jacobian, columns, innovation, inv_error)
-    outgoing = jnp.zeros((slots, width), jnp.bfloat16).at[slot].set(column_grad.astype(jnp.bfloat16))
+    wide = column_grad.shape[1]
+    outgoing = jnp.zeros((slots, wide), jnp.bfloat16).at[slot].set(column_grad)
     arrived = lax.all_to_all(
-        outgoing.reshape(devices, slots_each, width), ("lat", "lon"), split_axis=0, concat_axis=0, tiled=True
-    ).reshape(slots, width)
+        outgoing.reshape(devices, slots_each, wide), ("lat", "lon"), split_axis=0, concat_axis=0, tiled=True
+    ).reshape(slots, wide)
     near = jnp.concatenate([arrived, *around(arrived, "lat", False)], axis=0)
     grads = (near, *around(near, "lon", True))
     order = (0, -1, 1)

time: 189 us -> 188 us (level)
    ppermute x2 -> x0, local copies, waits for them, and re-layouts: 2.4 us -> none  [around(): return (lax.ppermute(array, axis, up), lax.ppermute(array, axis, down))]
    unnamed x45 -> x49, local copies, waits for them, and re-layouts: 5.04 us -> 6.79 us
where the time goes in v3:
time: 188 us
  Pallas kernels  68.5 us (36%)
  waiting for transfers between devices  55.1 us (29%)
  local copies, waits for them, and re-layouts  25.8 us (14%)
  starting transfers between devices  14.1 us (8%)
  matrix products  12.5 us (7%)
  other arithmetic  8.94 us (5%)
  between operations  2.54 us (1%)
    pallas_call x1, Pallas kernels, exchange(): pl.pallas_call(functools.partial(exchange_kernel, lat, lon, cuts), in_spe...  40.6 us
    ppermute x4, waiting for transfers between devices, around(): return (lax.ppermute(array, axis, up), lax.ppermute(array, axis, down))  23.6 us
    pallas_call x1, Pallas kernels, sounding_step(): pl.pallas_call(functools.partial(sounding_kernel, channels, step), grid=(...  16.7 us
    all_to_all x1, waiting for transfers between devices, local(): lax.all_to_all(outgoing.reshape(devices, slots_each, wide), ('lat', 'lon'...  11.8 us
    all_to_all x1, waiting for transfers between devices, local(): lax.all_to_all(picked.reshape(devices, slots_each, width), ('lat', 'lon')...  11.3 us
    pallas_call x1, Pallas kernels, adjoint_step(): pl.pallas_call(adjoint_kernel, grid=(lat_rows,), in_specs=[whole, whole,...  11.3 us
    unnamed x49, local copies, waits for them, and re-layouts  6.79 us
    ppermute x4, starting transfers between devices, around(): return (lax.ppermute(array, axis, up), lax.ppermute(array, axis, down))  6.59 us
  transfers between devices with their start and end apart: 8, of which 7 were waited for; matrix products, arithmetic and copies ran while one was open for 6% of the time, Pallas kernels for 0%

profile of v3, /device:TPU:0, one launch (start us, length us, event | category | flops | bytes accessed | tf_op | source)
XLA Modules:
  0.0 187.6 jit_solution(815949851321321149)
XLA Ops:
  2.0 2.7 %convert_element_type.74.tile_ref = bf16[548,8,128]{2,1,0:T(8,128)(2,1)} convert(f32[548,8,128]{2,1,0:T(8,128)} %param.8) | non-fusion elementwise | flops 561152 | bytes 3366912 | tf_op jit(solution)/shard_map/convert_element_type | solution.py:318
  4.9 1.0 scatter_custom_fusion
  6.5 40.6 %exchange.1 = (bf16[548,8,128]{2,1,0:T(8,128)(2,1)}, bf16[548,8,128]{2,1,0:T(8,128)(2,1)}, s32[32,1,256]{2,1,0:T(1,128)}) custom-call(bf16[548,8,128]{2,1,0:T(8,128)(2,1)} %convert_element_type.74.tile_ref, s32[1,1,256]{2,1,0:T(1,128)} %bitcast.60), custom_call_target="tpu_custom_call" | custom-call | tf_op jit(solution)/shard_map/exchange/pallas_call | solution.py:184
  47.1 1.5 convert_element_type.79
  48.9 1.4 copy-done
  50.3 3.5 %bitcast_convert_fusion = (bf16[548,8,128]{2,1,0:T(8,128)(2,1)S(1)}, f32[548,128,8]{1,2,0:T(8,128)S(1)}) fusion(f32[8,8]{1,0:T(8,128)S(1)} %get-tuple-element.55, f32[8,8]{1,0:T(8,128)S(1)} %get-tuple-element.54, f32[8,8]{1,0:T(8,128)S(1)} %get-tuple-element.53, f32[548,8,128]{2,1,0:T(8,128)S(1)} %convert_element_type.79, f32[548,8,128]{2,1,0:T(8,128)S(1)} %copy-done, ...), kind=kOutput, calls=%fused_computation.14 | convolution fusion | flops 165540224 | bytes 10101504 | tf_op jit(solution)/shard_map/ij,cjk->cik/dot_general | solution.py:58
  57.4 2.3 %constant_dynamic-slice_fusion.7 = (s32[32,1,6]{2,1,0:T(1,128)}, s32[32,1,6]{2,1,0:T(1,128)}, s32[32,1,6]{2,1,0:T(1,128)}, s32[32,1,6]{2,1,0:T(1,128)}, s32[32,1...) fusion(s32[32,1,192]{2,1,0:T(1,128)S(1)} %bitcast.48, ...), kind=kLoop, calls=%fused_computation.102 | loop fusion | bytes 14632 | tf_op jit(solution)/shard_map/dynamic_slice | solution.py:325
  60.7 6.5 %collective-permute-done.1 = bf16[274,8,128]{2,1,0:T(8,128)(2,1)} collective-permute-done((bf16[274,8,128]{2,1,0:T(8,128)(2,1)S(1)}, bf16[274,8,128]{2,1,0:T(8,128)(2,1)}, u32[]{:S(2)}, u32[]{:S(2)}) %collective-permute-start.1) | collective-permute-done | bytes 561184 | tf_op jit(solution)/shard_map/ppermute | solution.py:64
  67.1 1.9 %collective-permute-done = bf16[274,8,128]{2,1,0:T(8,128)(2,1)} collective-permute-done((bf16[274,8,128]{2,1,0:T(8,128)(2,1)S(1)}, bf16[274,8,128]{2,1,0:T(8,128)(2,1)}, u32[]{:S(2)}, u32[]{:S(2)}) %collective-permute-start) | collective-permute-done | bytes 561184 | tf_op jit(solution)/shard_map/ppermute | solution.py:63
  69.1 1.7 fusion.13
  70.7 1.7 convolution_add_fusion.1
  73.1 5.5 %bitcast_multiply_fusion = (f32[548,8,128]{2,1,0:T(8,128)}, f32[4384,128]{1,0:T(8,128)}) fusion(f32[548]{0:T(1024)S(1)} %copy-done.16, f32[2192,128]{1,0:T(8,128)S(1)} %get-tuple-element.34, f32[2192,128]{1,0:T(8,128)S(1)} %get-tuple-element.33, f32[256,128]{1,0:T(8,128)S(1)} %fusion.19, f32[548,128,8]{1,2,0:T(8,128)S(1)} %get-tuple-element.57), kind=kOutput, calls=%fused_computation.13 | convolution fusion | flops 863612928 | bytes 9048064 | tf_op jit(solution)/shard_map/dot_general | solution.py:73
  78.6 2.4 %reshape.334 = f32[548,1024]{1,0:T(8,128)S(1)} reshape(f32[4384,128]{1,0:T(8,128)} %get-tuple-element.59) | data formatting | bytes 4489216 | tf_op jit(solution)/shard_map/reshape | solution.py:76
  81.9 1.0 gather_fusion
  83.9 4.2 %all-to-all-start = ((bf16[32,6,548]{2,1,0:T(8,128)(2,1)}), bf16[32,6,548]{2,1,0:T(8,128)(2,1)S(1)}, u32[]{:S(2)}, u32[]{:S(2)}) async-start(bf16[32,6,548]{2,1,0:T(8,128)(2,1)} %reshape.336), calls=%async_computation | async-start | bytes 655360 | tf_op jit(solution)/shard_map/all_to_all | solution.py:332
  88.9 11.3 %all-to-all-done = bf16[32,6,548]{2,1,0:T(8,128)(2,1)S(1)} async-done(((bf16[32,6,548]{2,1,0:T(8,128)(2,1)}), bf16[32,6,548]{2,1,0:T(8,128)(2,1)S(1)}, u32[]{:S(2)}, u32[]{:S(2)}) %all-to-all-start) | async-done | bytes 210464 | tf_op jit(solution)/shard_map/all_to_all | solution.py:332
  100.3 1.4 gather_fusion.1
  101.8 16.7 %soundings.1 = (f32[96,256]{1,0:T(8,128)}, bf16[96,640]{1,0:T(8,128)(2,1)}) custom-call(bf16[150,96,548]{2,1,0:T(8,128)(2,1)} %bitcast.45, bf16[96,548]{1,0:T(8,128)(2,1)} %gather_fusion.1, f32[96,256]{1,0:T(8,128)} %pad.17.innov_ref, f32[1,150]{1,0:T(1,128)} %bitcast.62), custom_call_target="tpu_custom_call" | custom-call | tf_op jit(solution)/shard_map/soundings/pallas_call | solution.py:242
  118.5 1.4 scatter_custom_fusion.1
  120.7 2.7 %all-to-all-start.1 = ((bf16[32,6,640]{2,1,0:T(8,128)(2,1)}), bf16[32,6,640]{2,1,0:T(8,128)(2,1)S(1)}, u32[]{:S(2)}, u32[]{:S(2)}) async-start(bf16[32,6,640]{2,1,0:T(8,128)(2,1)} %reshape.339), calls=%async_computation.1 | async-start | bytes 655360 | tf_op jit(solution)/shard_map/all_to_all | solution.py:339
  123.7 11.8 %all-to-all-done.1 = bf16[32,6,640]{2,1,0:T(8,128)(2,1)S(1)} async-done(((bf16[32,6,640]{2,1,0:T(8,128)(2,1)}), bf16[32,6,640]{2,1,0:T(8,128)(2,1)S(1)}, u32[]{:S(2)}, u32[]{:S(2)}) %all-to-all-start.1) | async-done | bytes 245792 | tf_op jit(solution)/shard_map/all_to_all | solution.py:339
  135.6 1.7 collective-permute-start.2
  137.5 1.3 collective-permute-start.3
  139.2 4.2 %collective-permute-done.2 = bf16[192,640]{1,0:T(8,128)(2,1)S(1)} collective-permute-done((bf16[192,640]{1,0:T(8,128)(2,1)S(1)}, bf16[192,640]{1,0:T(8,128)(2,1)S(1)}, u32[]{:S(2)}, u32[]{:S(2)}) %collective-permute-start.2) | collective-permute-done | bytes 245792 | tf_op jit(solution)/shard_map/ppermute | solution.py:37
  143.4 7.6 %collective-permute-done.3 = bf16[192,640]{1,0:T(8,128)(2,1)S(1)} collective-permute-done((bf16[192,640]{1,0:T(8,128)(2,1)S(1)}, bf16[192,640]{1,0:T(8,128)(2,1)S(1)}, u32[]{:S(2)}, u32[]{:S(2)}) %collective-permute-start.3) | collective-permute-done | bytes 245792 | tf_op jit(solution)/shard_map/ppermute | solution.py:37
  151.1 3.5 %collective-permute-start.5 = (bf16[576,640]{1,0:T(8,128)(2,1)S(1)}, bf16[576,640]{1,0:T(8,128)(2,1)S(1)}, u32[]{:S(2)}, u32[]{:S(2)}) collective-permute-start(bf16[576,640]{1,0:T(8,128)(2,1)S(1)} %constant_dynamic-update-slice_fusion.near_ref), channel_id=1, source_target_pairs={{1,0},{2,1},{3,2},{4,3},{5,4},{6,5},{7,6},{0,7},{9,8},{10,9},{11,1... | collective-permute-start | bytes 2211848 | tf_op jit(solution)/shard_map/ppermute | solution.py:37
  157.0 1.3 fusion.12.col_ref
  159.1 11.8 %collective-permute-done.4.before_ref = bf16[576,640]{1,0:T(8,128)(2,1)S(1)} collective-permute-done((bf16[576,640]{1,0:T(8,128)(2,1)S(1)}, bf16[576,640]{1,0:T(8,128)(2,1)S(1)}, u32[]{:S(2)}, u32[]{:S(2)}) %collective-permute-start.4) | collective-permute-done | bytes 737312 | tf_op jit(solution)/shard_map/ppermute | solution.py:37
  170.9 0.9 copy-done.3
  172.6 11.3 %adjoint.1 = f32[548,1024]{1,0:T(8,128)} custom-call(bf16[576,640]{1,0:T(8,128)(2,1)} %copy-done.1, bf16[576,640]{1,0:T(8,128)(2,1)} %copy-done.3, bf16[576,640]{1,0:T(8,128)(2,1)} %copy-done.4, f32[3,128,576]{2,1,0:T(8,128)} %fusion.12.col_ref, f32[8,3,1,576]{3,2,1,0:T(1,128)} %compare_select_fusion.row_ref, f32[1,640]{1,0:T(1,128)} %broadcast_in_dim.65.std_ref), custom_call_target="tpu_custom_call" | custom-call | tf_op jit(solution)/shard_map/adjoint/pallas_call | solution.py:285
  183.9 2.1 %copy.77 = f32[69,8,8,128]{3,2,1,0:T(8,128)S(1)} copy(f32[69,8,8,128]{3,1,2,0:T(8,128)} %bitcast.46) | data formatting | bytes 4521984
  186.0 1.5 slice.75
  (104 shorter events, 14.6 us)
Async XLA Ops:
  0.6 4.1 %copy-start.21 = (s32[96,1]{0,1:T(1,128)S(1)}, s32[96,1]{0,1:T(1,128)}, u32[]{:S(2)}) copy-start(s32[96,1]{0,1:T(1,128)} %param.10) | copy-start | bytes 1156
  4.9 43.7 %copy-start.19 = (s32[96]{0:T(128)}, s32[96]{0:T(128)S(1)}, u32[]{:S(2)}) copy-start(s32[96]{0:T(128)S(1)} %fusion.45) | copy-start | bytes 1156
  47.1 1.6 copy-start.2
  48.6 1.7 copy-start
  54.2 3.2 %copy-start.5 = (s32[32,1,256]{2,1,0:T(1,128)S(1)}, s32[32,1,256]{2,1,0:T(1,128)}, u32[]{:S(2)}) copy-start(s32[32,1,256]{2,1,0:T(1,128)} %get-tuple-element.8) | copy-start | bytes 98308
  54.5 12.6 %collective-permute-start.1 = (bf16[274,8,128]{2,1,0:T(8,128)(2,1)S(1)}, bf16[274,8,128]{2,1,0:T(8,128)(2,1)}, u32[]{:S(2)}, u32[]{:S(2)}) collective-permute-start(bf16[274,8,128]{2,1,0:T(8,128)(2,1)S(1)} %pad_maximum_fusion.1), channel_id=1, source_target_pairs={{1,0},{2,1},{3,2},{4,3},{5,4},{6,5},{7,6},{0,7},{9,8},{10,9},{11,1... | collective-permute-start | bytes 1683464 | tf_op jit(solution)/shard_map/ppermute | solution.py:64
  54.9 14.1 %collective-permute-start = (bf16[274,8,128]{2,1,0:T(8,128)(2,1)S(1)}, bf16[274,8,128]{2,1,0:T(8,128)(2,1)}, u32[]{:S(2)}, u32[]{:S(2)}) collective-permute-start(bf16[274,8,128]{2,1,0:T(8,128)(2,1)S(1)} %pad_maximum_fusion), channel_id=1, source_target_pairs={{0,1},{1,2},{2,3},{3,4},{4,5},{5,6},{6,7},{7,0},{8,9},{9,10},{10,1... | collective-permute-start | bytes 1683464 | tf_op jit(solution)/shard_map/ppermute | solution.py:63
  72.4 0.7 copy-start.16
  81.9 6.2 %copy-start.7 = (f32[96,150]{0,1:T(8,128)S(1)}, f32[96,150]{0,1:T(8,128)}, u32[]{:S(2)}) copy-start(f32[96,150]{0,1:T(8,128)} %param.13) | copy-start | bytes 172804
  81.9 7.0 %copy-start.20 = (s32[96]{0:T(128)S(1)}, s32[96]{0:T(128)}, u32[]{:S(2)}) copy-start(s32[96]{0:T(128)} %copy-done.19) | copy-start | bytes 1156
  83.9 16.3 %all-to-all-start = ((bf16[32,6,548]{2,1,0:T(8,128)(2,1)}), bf16[32,6,548]{2,1,0:T(8,128)(2,1)S(1)}, u32[]{:S(2)}, u32[]{:S(2)}) async-start(bf16[32,6,548]{2,1,0:T(8,128)(2,1)} %reshape.336), calls=%async_computation | async-start | bytes 655360 | tf_op jit(solution)/shard_map/all_to_all | solution.py:332
  101.8 21.7 %copy-start.15 = (s32[32,1,6]{2,1,0:T(1,128)S(1)}, s32[32,1,6]{2,1,0:T(1,128)}, u32[]{:S(2)}) copy-start(s32[32,1,6]{2,1,0:T(1,128)} %get-tuple-element.42) | copy-start | bytes 2308
  101.8 21.8 %copy-start.14 = (s32[32,1,6]{2,1,0:T(1,128)S(1)}, s32[32,1,6]{2,1,0:T(1,128)}, u32[]{:S(2)}) copy-start(s32[32,1,6]{2,1,0:T(1,128)} %get-tuple-element.43) | copy-start | bytes 2308
  101.8 21.8 %copy-start.13 = (s32[32,1,6]{2,1,0:T(1,128)S(1)}, s32[32,1,6]{2,1,0:T(1,128)}, u32[]{:S(2)}) copy-start(s32[32,1,6]{2,1,0:T(1,128)} %get-tuple-element.44) | copy-start | bytes 2308
  101.8 35.5 %copy-start.12 = (s32[32,1,6]{2,1,0:T(1,128)S(1)}, s32[32,1,6]{2,1,0:T(1,128)}, u32[]{:S(2)}) copy-start(s32[32,1,6]{2,1,0:T(1,128)} %get-tuple-element.45) | copy-start | bytes 2308
  101.8 35.6 %copy-start.11 = (s32[32,1,6]{2,1,0:T(1,128)S(1)}, s32[32,1,6]{2,1,0:T(1,128)}, u32[]{:S(2)}) copy-start(s32[32,1,6]{2,1,0:T(1,128)} %get-tuple-element.46) | copy-start | bytes 2308
  101.8 35.7 %copy-start.10 = (s32[32,1,6]{2,1,0:T(1,128)S(1)}, s32[32,1,6]{2,1,0:T(1,128)}, u32[]{:S(2)}) copy-start(s32[32,1,6]{2,1,0:T(1,128)} %get-tuple-element.47) | copy-start | bytes 2308
  118.5 20.5 %copy-start.9 = (s32[32,1,6]{2,1,0:T(1,128)S(1)}, s32[32,1,6]{2,1,0:T(1,128)}, u32[]{:S(2)}) copy-start(s32[32,1,6]{2,1,0:T(1,128)} %get-tuple-element.48) | copy-start | bytes 2308
  118.5 20.6 %copy-start.8 = (s32[32,1,6]{2,1,0:T(1,128)S(1)}, s32[32,1,6]{2,1,0:T(1,128)}, u32[]{:S(2)}) copy-start(s32[32,1,6]{2,1,0:T(1,128)} %get-tuple-element.41) | copy-start | bytes 2308
  118.5 36.9 %copy-start.18 = (s32[3]{0:T(128)S(1)}, s32[3]{0:T(128)}, u32[]{:S(2)}) copy-start(s32[3]{0:T(128)} %constant.176) | copy-start | bytes 40
  118.5 37.7 %copy-start.17 = (s32[3]{0:T(128)S(1)}, s32[3]{0:T(128)}, u32[]{:S(2)}) copy-start(s32[3]{0:T(128)} %constant.175) | copy-start | bytes 40
  120.7 37.6 %copy-start.6 = (f32[96,256]{1,0:T(8,128)S(1)}, f32[96,256]{1,0:T(8,128)}, u32[]{:S(2)}) copy-start(f32[96,256]{1,0:T(8,128)} %get-tuple-element.11) | copy-start | bytes 294916
  120.7 14.8 %all-to-all-start.1 = ((bf16[32,6,640]{2,1,0:T(8,128)(2,1)}), bf16[32,6,640]{2,1,0:T(8,128)(2,1)S(1)}, u32[]{:S(2)}, u32[]{:S(2)}) async-start(bf16[32,6,640]{2,1,0:T(8,128)(2,1)} %reshape.339), calls=%async_computation.1 | async-start | bytes 655360 | tf_op jit(solution)/shard_map/all_to_all | solution.py:339
  135.6 7.8 %collective-permute-start.2 = (bf16[192,640]{1,0:T(8,128)(2,1)S(1)}, bf16[192,640]{1,0:T(8,128)(2,1)S(1)}, u32[]{:S(2)}, u32[]{:S(2)}) collective-permute-start(bf16[192,640]{1,0:T(8,128)(2,1)S(1)} %reshape.340), channel_id=1, source_target_pairs={{0,8},{8,16},{16,24},{1,9},{9,17},{17,25},{2,10},{10,18},{18,26},{... | collective-permute-start | bytes 737288 | tf_op jit(solution)/shard_map/ppermute | solution.py:37
  137.5 13.4 %collective-permute-start.3 = (bf16[192,640]{1,0:T(8,128)(2,1)S(1)}, bf16[192,640]{1,0:T(8,128)(2,1)S(1)}, u32[]{:S(2)}, u32[]{:S(2)}) collective-permute-start(bf16[192,640]{1,0:T(8,128)(2,1)S(1)} %reshape.340), channel_id=1, source_target_pairs={{8,0},{16,8},{24,16},{9,1},{17,9},{25,17},{10,2},{18,10},{26,18},{... | collective-permute-start | bytes 737288 | tf_op jit(solution)/shard_map/ppermute | solution.py:37
  151.0 19.9 %copy-start.1 = (bf16[576,640]{1,0:T(8,128)(2,1)}, bf16[576,640]{1,0:T(8,128)(2,1)S(1)}, u32[]{:S(2)}) copy-start(bf16[576,640]{1,0:T(8,128)(2,1)S(1)} %constant_dynamic-update-slice_fusion.near_ref) | copy-start | bytes 2211844
  151.0 19.9 %collective-permute-start.4 = (bf16[576,640]{1,0:T(8,128)(2,1)S(1)}, bf16[576,640]{1,0:T(8,128)(2,1)S(1)}, u32[]{:S(2)}, u32[]{:S(2)}) collective-permute-start(bf16[576,640]{1,0:T(8,128)(2,1)S(1)} %constant_dynamic-update-slice_fusion.near_ref), channel_id=1, source_target_pairs={{0,1},{1,2},{2,3},{3,4},{4,5},{5,6},{6,7},{7,0},{8,9},{9,10},{10,1... | collective-permute-start | bytes 2211848 | tf_op jit(solution)/shard_map/ppermute | solution.py:37
  151.1 19.8 %collective-permute-start.5 = (bf16[576,640]{1,0:T(8,128)(2,1)S(1)}, bf16[576,640]{1,0:T(8,128)(2,1)S(1)}, u32[]{:S(2)}, u32[]{:S(2)}) collective-permute-start(bf16[576,640]{1,0:T(8,128)(2,1)S(1)} %constant_dynamic-update-slice_fusion.near_ref), channel_id=1, source_target_pairs={{1,0},{2,1},{3,2},{4,3},{5,4},{6,5},{7,6},{0,7},{9,8},{10,9},{11,1... | collective-permute-start | bytes 2211848 | tf_op jit(solution)/shard_map/ppermute | solution.py:37
  170.9 0.9 copy-start.3
  171.8 0.9 copy-start.4
